TPU v7x, 32 devices: a whole 2x2x4 slice. The times are simulated.
32 devices in a mesh: gx: 8 (over z, core), gy: 4 (over y, x).
Axes of the slice: x: 2, y: 2, z: 4, core: 2. Of those that a mesh axis runs over, the one named last changes fastest.
Arguments:
- theta: float32 [32, 1024, 1024], P('gx', 'gy'), may hold values from 0.9 to 1.4
- pressure: float32 [32, 1024, 1024], P('gx', 'gy'), may hold values from 0.1 to 1
- vertical_wind: float32 [32, 1024, 1024], P('gx', 'gy'), may hold values from -6 to 6
- terrain: float32 [1024, 1024], P('gx', 'gy'), may hold values from 0 to 0.5
- column_mass: float32 [1024, 1024], P('gx', 'gy'), may hold values from 0.5 to 1
- land_mask: int32 [1024, 1024], P('gx', 'gy'), may hold values 0 or 1
- pbl_top: int32 [1024, 1024], P('gx', 'gy'), may hold values from 2 to 27
Outputs:
- updated_wind: float32 [32, 1024, 1024], P(None, 'gx', 'gy')
- geopotential: float32 [32, 1024, 1024], P(None, 'gx', 'gy')
All inputs are finite; a program needn't handle non-finite values. No bound on the sum of `land_mask` on one device may be relied on, other than what follows from the above.
Results may differ from a plain program's by a relative error of at most 0.00002.
Values sent between devices are 32-bit elements; how exact they have to be, the bound alone decides.
No kernel may reach another device: no remote copies, remote signals or barrier semaphores. Data moves between devices by JAX's collectives and lax.ppermute only.
A program may use at most 128 MiB of HBM per device.

v0:
```python
import jax
import jax.numpy as jnp
from jax import lax
from jax.sharding import PartitionSpec as P

gamma_ratio = 1.4
smooth_rate = 0.2
lift_rate = 0.3
couple_rate = 0.5
land_boost = 0.5


def extended(x, sides, width):
    for axis, dim in sides:
        count, length = (lax.axis_size(axis), x.shape[dim])
        up = [(i, (i + 1) % count) for i in range(count - 1)]
        down = [(j, i) for i, j in up]
        last = lax.slice_in_dim(x, length - width, length, axis=dim)
        initial = lax.slice_in_dim(x, 0, width, axis=dim)
        before = lax.ppermute(last, axis, up)
        after = lax.ppermute(initial, axis, down)
        x = jnp.concatenate([before, x, after], axis=dim)
    return x


def states(theta, pressure):
    alpha = theta * jnp.exp(-jnp.log(pressure) / gamma_ratio)
    sound_sq = gamma_ratio * pressure * alpha
    return (alpha, sound_sq)


def heights(terrain, column_mass, rising):
    return terrain[None] + column_mass[None] * rising / rising.shape[0]


def laplacian(padded):
    middle = padded[..., 1:-1, 1:-1]
    return (
        padded[..., 2:, 1:-1]
        + padded[..., :-2, 1:-1]
        + padded[..., 1:-1, 2:]
        + padded[..., 1:-1, :-2]
        - 4.0 * middle
    )


def column_solve(forcing, sound_sq, land_mask, pbl_top):
    levels = lax.broadcasted_iota(jnp.int32, forcing.shape, 0)
    inside = (land_mask[None] > 0) & (levels < pbl_top[None])
    damping = jnp.where(inside, 1.0 + land_boost, 1.0).astype(jnp.float32)
    couple = couple_rate * 0.5 * (sound_sq[:-1] + sound_sq[1:])
    zero_level = jnp.zeros_like(forcing[:1])
    below = jnp.concatenate([zero_level, couple], 0)
    above = jnp.concatenate([couple, zero_level], 0)
    centre = damping + below + above
    count = forcing.shape[0]
    ratios = []
    values = []
    ratio = above[0] / centre[0]
    value = forcing[0] / centre[0]
    ratios.append(ratio)
    values.append(value)
    for level in range(1, count):
        denom = centre[level] - below[level] * ratio
        value = (forcing[level] + below[level] * value) / denom
        ratio = above[level] / denom
        ratios.append(ratio)
        values.append(value)
    result = [None] * count
    current = values[count - 1]
    result[count - 1] = current
    for level in range(count - 2, -1, -1):
        current = values[level] + ratios[level] * current
        result[level] = current
    return jnp.stack(result, 0)


def on_device(theta, pressure, vertical_wind, terrain, column_mass, land_mask, pbl_top):
    theta_col, press_col, wind_col = (
        lax.all_to_all(
            lax.all_to_all(theta, "gy", split_axis=2, concat_axis=1, tiled=True),
            "gx",
            split_axis=1,
            concat_axis=0,
            tiled=True,
        ),
        lax.all_to_all(
            lax.all_to_all(pressure, "gy", split_axis=2, concat_axis=1, tiled=True),
            "gx",
            split_axis=1,
            concat_axis=0,
            tiled=True,
        ),
        lax.all_to_all(
            lax.all_to_all(vertical_wind, "gy", split_axis=2, concat_axis=1, tiled=True),
            "gx",
            split_axis=1,
            concat_axis=0,
            tiled=True,
        ),
    )
    alpha, sound_sq = states(theta_col, press_col)
    rising = jnp.cumsum(alpha, axis=0)
    wind_pad = extended(wind_col, (("gx", 1), ("gy", 2)), 1)
    geopotential = heights(terrain, column_mass, rising)
    geo_pad = extended(geopotential, (("gx", 1), ("gy", 2)), 1)
    forcing = wind_col + smooth_rate * laplacian(wind_pad) + lift_rate * laplacian(geo_pad)
    updated_wind = column_solve(forcing, sound_sq, land_mask, pbl_top)
    return (updated_wind, geopotential)


def solution(mesh):
    placed = (
        P("gx", "gy", None),
        P("gx", "gy", None),
        P("gx", "gy", None),
        P("gx", "gy"),
        P("gx", "gy"),
        P("gx", "gy"),
        P("gx", "gy"),
    )
    return jax.shard_map(
        on_device,
        mesh=mesh,
        in_specs=placed,
        out_specs=(P(None, "gx", "gy"), P(None, "gx", "gy")),
        check_vma=False,
    )
```

profile of v0, /device:TPU:12, one launch (start us, length us, event | category | flops | bytes accessed | tf_op | source)
XLA Modules:
  0.0 544.8 jit_solution(15851482188488028516)
XLA Ops:
  0.6 5.3 copy.31
  5.9 5.3 all-to-all-start.2
  11.2 5.2 copy.35
  16.4 41.9 %all-to-all-done.2 = f32[4,256,1024]{1,0,2:T(4,128)} async-done(((f32[4,256,1024]{1,0,2:T(4,128)}), f32[4,256,1024]{1,0,2:T(4,128)}, u32[]{:S(2)}, u32[]{:S(2)}) %all-to-all-start.2) | async-done | bytes 4194336 | tf_op jit(solution)/shard_map/all_to_all | solution.py:81
  58.4 5.4 all-to-all-start.4
  63.8 5.2 copy.21
  69.0 41.2 %all-to-all-done.4 = f32[4,256,1024]{1,0,2:T(4,128)} async-done(((f32[4,256,1024]{1,0,2:T(4,128)}), f32[4,256,1024]{1,0,2:T(4,128)}, u32[]{:S(2)}, u32[]{:S(2)}) %all-to-all-start.4) | async-done | bytes 4194336 | tf_op jit(solution)/shard_map/all_to_all | solution.py:88
  110.2 5.4 all-to-all-start
  115.6 5.0 copy.32
  120.6 5.2 copy.33
  125.9 6.9 %copy.34 = f32[4,1024,256]{2,0,1:T(4,128)} copy(f32[4,1024,256]{2,1,0:T(8,128)} %bitcast.32) | data formatting | bytes 8388608 | tf_op jit(solution)/shard_map/all_to_all | solution.py:81
  132.8 29.3 %all-to-all-done = f32[4,256,1024]{1,0,2:T(4,128)} async-done(((f32[4,256,1024]{1,0,2:T(4,128)}), f32[4,256,1024]{1,0,2:T(4,128)}, u32[]{:S(2)}, u32[]{:S(2)}) %all-to-all-start) | async-done | bytes 4194336 | tf_op jit(solution)/shard_map/all_to_all | solution.py:95
  162.0 5.3 all-to-all-start.3
  167.4 5.0 copy.36
  172.4 5.3 copy.37
  177.6 6.9 %copy.38 = f32[4,1024,256]{2,0,1:T(4,128)} copy(f32[4,1024,256]{2,1,0:T(8,128)} %bitcast.34) | data formatting | bytes 8388608 | tf_op jit(solution)/shard_map/all_to_all | solution.py:88
  184.5 73.4 %all-to-all-done.3 = f32[4,1024,256]{2,0,1:T(4,128)} async-done(((f32[4,1024,256]{2,0,1:T(4,128)}), f32[4,1024,256]{2,0,1:T(4,128)}, u32[]{:S(2)}, u32[]{:S(2)}) %all-to-all-start.3) | async-done | bytes 4194336 | tf_op jit(solution)/shard_map/all_to_all | solution.py:80
  257.9 8.0 %all-to-all-start.5 = ((f32[4,1024,256]{2,0,1:T(4,128)}), f32[4,1024,256]{2,0,1:T(4,128)}, u32[]{:S(2)}, u32[]{:S(2)}) async-start(f32[4,1024,256]{2,0,1:T(4,128)} %copy.38), calls=%async_computation.5 | async-start | bytes 8388608 | tf_op jit(solution)/shard_map/all_to_all | solution.py:87
  265.9 5.0 copy.22
  270.9 5.2 copy.23
  276.2 6.9 %copy.24 = f32[4,1024,256]{2,0,1:T(4,128)} copy(f32[4,1024,256]{2,1,0:T(8,128)} %bitcast.36) | data formatting | bytes 8388608 | tf_op jit(solution)/shard_map/all_to_all | solution.py:95
  283.1 73.4 %all-to-all-done.5 = f32[4,1024,256]{2,0,1:T(4,128)} async-done(((f32[4,1024,256]{2,0,1:T(4,128)}), f32[4,1024,256]{2,0,1:T(4,128)}, u32[]{:S(2)}, u32[]{:S(2)}) %all-to-all-start.5) | async-done | bytes 4194336 | tf_op jit(solution)/shard_map/all_to_all | solution.py:87
  356.5 8.0 %all-to-all-start.1 = ((f32[4,1024,256]{2,0,1:T(4,128)}), f32[4,1024,256]{2,0,1:T(4,128)}, u32[]{:S(2)}, u32[]{:S(2)}) async-start(f32[4,1024,256]{2,0,1:T(4,128)} %copy.24), calls=%async_computation.1 | async-start | bytes 8388608 | tf_op jit(solution)/shard_map/all_to_all | solution.py:94
  364.5 5.6 %copy_multiply_fusion = (f32[4,1024,256]{2,1,0:T(8,128)S(1)}, f32[4,1024,256]{2,1,0:T(8,128)S(1)}) fusion(f32[4,1024,256]{2,0,1:T(4,128)} %all-to-all-done.3, f32[4,1024,256]{2,0,1:T(4,128)} %all-to-all-done.5), kind=kLoop, calls=%fused_computation.31 | loop fusion | flops 4194304 | bytes 16777216 | tf_op jit(solution)/shard_map/mul | solution.py:27
  370.2 0.4 copy.41
  370.6 0.0 copy-start.3
  370.6 0.4 copy.47
  371.1 1.6 copy-done.3
  372.6 1.2 bitcast_multiply_fusion
  373.8 2.5 fusion.13
  376.3 78.7 %all-to-all-done.1 = f32[4,1024,256]{2,0,1:T(4,128)} async-done(((f32[4,1024,256]{2,0,1:T(4,128)}), f32[4,1024,256]{2,0,1:T(4,128)}, u32[]{:S(2)}, u32[]{:S(2)}) %all-to-all-start.1) | async-done | bytes 4194336 | tf_op jit(solution)/shard_map/all_to_all | solution.py:94
  455.0 3.0 copy.25
  458.0 0.0 copy-start.4
  458.0 0.0 copy-start.6
  458.1 0.0 copy-start.7
  458.1 0.4 copy.26
  458.6 2.4 collective-permute-start.1
  461.0 4.6 collective-permute-start
  465.6 0.6 multiply_add_fusion
  466.2 0.0 copy-start.1
  466.3 1.9 collective-permute-start.5
  468.2 3.9 collective-permute-start.4
  472.1 0.5 pad_maximum_fusion
  472.6 2.1 fusion.75
  474.7 2.8 copy.27
  477.5 1.2 copy.29
  478.7 2.4 collective-permute-start.3
  481.1 4.3 collective-permute-start.2
  485.5 2.6 pad_maximum_fusion.1
  488.1 2.1 fusion.76
  490.1 2.9 copy.42
  493.0 1.2 copy.44
  494.2 1.9 collective-permute-start.7
  496.1 4.8 collective-permute-start.6
  501.0 6.6 %pad_add_fusion = f32[32,128,256]{2,1,0:T(8,128)} fusion(f32[31,128,256]{2,1,0:T(8,128)} %fusion.13, s32[128,256]{1,0:T(8,128)S(1)} %copy-done.8, pred[128,256]{1,0:T(8,128)(4,1)S(1)} %broadcast_compare_fusion), kind=kLoop, calls=%fused_computation.32 | loop fusion | flops 5242880 | bytes 8421376 | tf_op jit(solution)/shard_map/add | solution.py:55
  507.6 0.7 copy.28
  508.3 2.1 copy.30
  510.4 2.2 copy.43
  512.6 2.2 copy.45
  514.8 24.9 %fusion.3 = f32[32,128,256]{2,1,0:T(8,128)S(1)} fusion(f32[32,130,1]{2,1,0:T(8,128)} %copy.45, f32[32,1,256]{2,1,0:T(1,128)S(1)} %collective-permute-done.4, f32[32,128,256]{2,1,0:T(8,128)} %copy-done.1, f32[32,1,256]{2,1,0:T(1,128)S(1)} %collective-permute-done.5, f32[32,130,1]{2,1,0:T(8,128)} %copy.43, f32[32,128,256]{2,1,0:T(8,128)} %bitcast.29, ...), kind=kLoop, calls=%fused_computation.6 | loop fusion | flops 31457280 | bytes 12780544 | tf_op jit(solution)/shard_map/add | solution.py:107
  539.7 1.5 fusion.16
  541.2 0.8 add_dynamic-update-slice_fusion
  542.8 0.0 copy-start.10
  542.8 2.0 copy-done.10
  (56 shorter events, 0.8 us)
Async XLA Ops:
  5.9 52.5 %all-to-all-start.2 = ((f32[4,256,1024]{1,0,2:T(4,128)}), f32[4,256,1024]{1,0,2:T(4,128)}, u32[]{:S(2)}, u32[]{:S(2)}) async-start(f32[4,256,1024]{1,0,2:T(4,128)} %copy.31), calls=%async_computation.2 | async-start | bytes 8388608 | tf_op jit(solution)/shard_map/all_to_all | solution.py:81
  58.4 51.8 %all-to-all-start.4 = ((f32[4,256,1024]{1,0,2:T(4,128)}), f32[4,256,1024]{1,0,2:T(4,128)}, u32[]{:S(2)}, u32[]{:S(2)}) async-start(f32[4,256,1024]{1,0,2:T(4,128)} %copy.35), calls=%async_computation.4 | async-start | bytes 8388608 | tf_op jit(solution)/shard_map/all_to_all | solution.py:88
  110.2 51.8 %all-to-all-start = ((f32[4,256,1024]{1,0,2:T(4,128)}), f32[4,256,1024]{1,0,2:T(4,128)}, u32[]{:S(2)}, u32[]{:S(2)}) async-start(f32[4,256,1024]{1,0,2:T(4,128)} %copy.21), calls=%async_computation | async-start | bytes 8388608 | tf_op jit(solution)/shard_map/all_to_all | solution.py:95
  162.0 95.9 %all-to-all-start.3 = ((f32[4,1024,256]{2,0,1:T(4,128)}), f32[4,1024,256]{2,0,1:T(4,128)}, u32[]{:S(2)}, u32[]{:S(2)}) async-start(f32[4,1024,256]{2,0,1:T(4,128)} %copy.34), calls=%async_computation.3 | async-start | bytes 8388608 | tf_op jit(solution)/shard_map/all_to_all | solution.py:80
  257.9 98.6 %all-to-all-start.5 = ((f32[4,1024,256]{2,0,1:T(4,128)}), f32[4,1024,256]{2,0,1:T(4,128)}, u32[]{:S(2)}, u32[]{:S(2)}) async-start(f32[4,1024,256]{2,0,1:T(4,128)} %copy.38), calls=%async_computation.5 | async-start | bytes 8388608 | tf_op jit(solution)/shard_map/all_to_all | solution.py:87
  283.1 81.4 %copy-start.9 = (s32[128,256]{1,0:T(8,128)S(1)}, s32[128,256]{1,0:T(8,128)}, u32[]{:S(2)}) copy-start(s32[128,256]{1,0:T(8,128)} %param.12) | copy-start | bytes 393220
  356.5 98.6 %all-to-all-start.1 = ((f32[4,1024,256]{2,0,1:T(4,128)}), f32[4,1024,256]{2,0,1:T(4,128)}, u32[]{:S(2)}, u32[]{:S(2)}) async-start(f32[4,1024,256]{2,0,1:T(4,128)} %copy.24), calls=%async_computation.1 | async-start | bytes 8388608 | tf_op jit(solution)/shard_map/all_to_all | solution.py:94
  370.6 2.0 copy-start.3
  458.0 7.5 %copy-start.4 = (f32[8,4,128,256]{3,2,1,0:T(8,128)S(1)}, f32[8,4,128,256]{3,2,1,0:T(8,128)}, u32[]{:S(2)}) copy-start(f32[8,4,128,256]{3,2,1,0:T(8,128)} %copy-done.3) | copy-start | bytes 12582916
  458.0 7.5 %copy-start.6 = (f32[128,256]{1,0:T(8,128)S(1)}, f32[128,256]{1,0:T(8,128)}, u32[]{:S(2)}) copy-start(f32[128,256]{1,0:T(8,128)} %param.11) | copy-start | bytes 393220
  458.1 7.5 %copy-start.7 = (f32[128,256]{1,0:T(8,128)S(1)}, f32[128,256]{1,0:T(8,128)}, u32[]{:S(2)}) copy-start(f32[128,256]{1,0:T(8,128)} %param.10) | copy-start | bytes 393220
  458.5 13.6 %copy-start.2 = (f32[8,4,128,256]{3,2,1,0:T(8,128)}, f32[8,4,128,256]{3,2,1,0:T(8,128)S(1)}, u32[]{:S(2)}) copy-start(f32[8,4,128,256]{3,2,1,0:T(8,128)S(1)} %copy.26) | copy-start | bytes 12582916
  458.6 13.5 %collective-permute-start.1 = (f32[32,1,256]{2,1,0:T(1,128)S(1)}, f32[32,1,256]{2,1,0:T(1,128)S(1)}, u32[]{:S(2)}, u32[]{:S(2)}) collective-permute-start(f32[32,1,256]{2,1,0:T(1,128)S(1)} %get-tuple-element.83), channel_id=1, source_target_pairs={{0,4},{4,8},{8,12},{12,16},{16,20},{20,24},{24,28},{1,5},{5,9},{9,... | collective-permute-start | bytes 98312 | tf_op jit(solution)/shard_map/ppermute | solution.py:20
  461.0 11.1 %collective-permute-start = (f32[32,1,256]{2,1,0:T(1,128)S(1)}, f32[32,1,256]{2,1,0:T(1,128)S(1)}, u32[]{:S(2)}, u32[]{:S(2)}) collective-permute-start(f32[32,1,256]{2,1,0:T(1,128)S(1)} %get-tuple-element.84), channel_id=1, source_target_pairs={{4,0},{8,4},{12,8},{16,12},{20,16},{24,20},{28,24},{5,1},{9,5},{13... | collective-permute-start | bytes 98312 | tf_op jit(solution)/shard_map/ppermute | solution.py:21
  466.2 6.4 %copy-start.1 = (f32[32,128,256]{2,1,0:T(8,128)}, f32[32,128,256]{2,1,0:T(8,128)S(1)}, u32[]{:S(2)}) copy-start(f32[32,128,256]{2,1,0:T(8,128)S(1)} %multiply_add_fusion) | copy-start | bytes 12582916
  466.3 19.2 %collective-permute-start.5 = (f32[32,1,256]{2,1,0:T(1,128)S(1)}, f32[32,1,256]{2,1,0:T(1,128)S(1)}, u32[]{:S(2)}, u32[]{:S(2)}) collective-permute-start(f32[32,1,256]{2,1,0:T(1,128)S(1)} %get-tuple-element.85), channel_id=1, source_target_pairs={{0,4},{4,8},{8,12},{12,16},{16,20},{20,24},{24,28},{1,5},{5,9},{9,... | collective-permute-start | bytes 98312 | tf_op jit(solution)/shard_map/ppermute | solution.py:20
  468.2 17.3 %collective-permute-start.4 = (f32[32,1,256]{2,1,0:T(1,128)S(1)}, f32[32,1,256]{2,1,0:T(1,128)S(1)}, u32[]{:S(2)}, u32[]{:S(2)}) collective-permute-start(f32[32,1,256]{2,1,0:T(1,128)S(1)} %get-tuple-element.86), channel_id=1, source_target_pairs={{4,0},{8,4},{12,8},{16,12},{20,16},{24,20},{28,24},{5,1},{9,5},{13... | collective-permute-start | bytes 98312 | tf_op jit(solution)/shard_map/ppermute | solution.py:21
  478.7 29.6 %collective-permute-start.3 = (f32[32,130,1]{1,0,2:T(8,128)S(1)}, f32[32,130,1]{1,0,2:T(8,128)S(1)}, u32[]{:S(2)}, u32[]{:S(2)}) collective-permute-start(f32[32,130,1]{1,0,2:T(8,128)S(1)} %copy.29), channel_id=1, source_target_pairs={{0,1},{1,2},{2,3},{4,5},{5,6},{6,7},{8,9},{9,10},{10,11},{12,13},{... | collective-permute-start | bytes 49928 | tf_op jit(solution)/shard_map/ppermute | solution.py:20
  481.1 26.5 %collective-permute-start.2 = (f32[32,130,1]{1,0,2:T(8,128)S(1)}, f32[32,130,1]{1,0,2:T(8,128)S(1)}, u32[]{:S(2)}, u32[]{:S(2)}) collective-permute-start(f32[32,130,1]{1,0,2:T(8,128)S(1)} %copy.27), channel_id=1, source_target_pairs={{1,0},{2,1},{3,2},{5,4},{6,5},{7,6},{9,8},{10,9},{11,10},{13,12},{... | collective-permute-start | bytes 49928 | tf_op jit(solution)/shard_map/ppermute | solution.py:21
  490.1 10.8 %copy-start.8 = (s32[128,256]{1,0:T(8,128)S(1)}, s32[128,256]{1,0:T(8,128)}, u32[]{:S(2)}) copy-start(s32[128,256]{1,0:T(8,128)} %param.13) | copy-start | bytes 393220
  494.2 18.4 %collective-permute-start.7 = (f32[32,130,1]{1,0,2:T(8,128)S(1)}, f32[32,130,1]{1,0,2:T(8,128)S(1)}, u32[]{:S(2)}, u32[]{:S(2)}) collective-permute-start(f32[32,130,1]{1,0,2:T(8,128)S(1)} %copy.44), channel_id=1, source_target_pairs={{0,1},{1,2},{2,3},{4,5},{5,6},{6,7},{8,9},{9,10},{10,11},{12,13},{... | collective-permute-start | bytes 49928 | tf_op jit(solution)/shard_map/ppermute | solution.py:20
  496.1 14.3 %collective-permute-start.6 = (f32[32,130,1]{1,0,2:T(8,128)S(1)}, f32[32,130,1]{1,0,2:T(8,128)S(1)}, u32[]{:S(2)}, u32[]{:S(2)}) collective-permute-start(f32[32,130,1]{1,0,2:T(8,128)S(1)} %copy.42), channel_id=1, source_target_pairs={{1,0},{2,1},{3,2},{5,4},{6,5},{7,6},{9,8},{10,9},{11,10},{13,12},{... | collective-permute-start | bytes 49928 | tf_op jit(solution)/shard_map/ppermute | solution.py:21
  514.8 24.9 %copy-start = (f32[31,128,256]{2,1,0:T(8,128)S(1)}, f32[31,128,256]{2,1,0:T(8,128)}, u32[]{:S(2)}) copy-start(f32[31,128,256]{2,1,0:T(8,128)} %fusion.13) | copy-start | bytes 12189700
  514.8 24.9 %copy-start.5 = (f32[32,128,256]{2,1,0:T(8,128)S(1)}, f32[32,128,256]{2,1,0:T(8,128)}, u32[]{:S(2)}) copy-start(f32[32,128,256]{2,1,0:T(8,128)} %pad_add_fusion) | copy-start | bytes 12582916
  542.8 2.0 copy-start.10
where the time goes:
time: 547 us; the launch traced here: 545 us
  waiting for transfers between devices  338 us (62%)
  local copies, waits for them, and re-layouts  94.8 us (17%)
  starting transfers between devices  63.8 us (12%)
  other arithmetic  47.2 us (9%)
    all_to_all x1, waiting for transfers between devices, on_device(): lax.all_to_all(lax.all_to_all(vertical_wind, 'gy', split_axis=2, concat_a...  78.7 us
    all_to_all x1, waiting for transfers between devices, on_device(): lax.all_to_all(lax.all_to_all(pressure, 'gy', split_axis=2, concat_axis=1...  73.4 us
    all_to_all x1, waiting for transfers between devices, on_device(): lax.all_to_all(lax.all_to_all(theta, 'gy', split_axis=2, concat_axis=1, t...  73.4 us
    all_to_all x1, waiting for transfers between devices, on_device(): lax.all_to_all(theta, 'gy', split_axis=2, concat_axis=1, tiled=True)  41.9 us
    all_to_all x1, waiting for transfers between devices, on_device(): lax.all_to_all(pressure, 'gy', split_axis=2, concat_axis=1, tiled=True)  41.2 us
    all_to_all x1, waiting for transfers between devices, on_device(): lax.all_to_all(vertical_wind, 'gy', split_axis=2, concat_axis=1, tiled=True)  29.3 us
    add x1, other arithmetic, on_device(): wind_col + smooth_rate * laplacian(wind_pad)  24.9 us
    unnamed x40, local copies, waits for them, and re-layouts  19.5 us
  transfers between devices with their start and end apart: 14, of which 6 were waited for; matrix products, arithmetic and copies ran while one was open for 18% of the time, Pallas kernels for 0%

commit v1 on v0

v1 whole, which is shorter than its diff:
```python
import jax
import jax.numpy as jnp
from jax import lax
from jax.experimental import pallas as pl
from jax.experimental.pallas import tpu as pltpu
from jax.sharding import PartitionSpec as P


gamma_ratio = 1.4
smooth_rate = 0.2
lift_rate = 0.3
couple_rate = 0.5
land_boost = 0.5


AXES = ("gx", "gy")
ANY = pl.BlockSpec(memory_space=pl.ANY)
SMEM = pl.BlockSpec(memory_space=pltpu.SMEM)
f32 = jnp.float32


def sds(*shape):
    return jax.ShapeDtypeStruct(shape, f32)


def states(theta, pressure):
    alpha = theta * jnp.exp(-jnp.log(pressure) / gamma_ratio)
    return alpha, gamma_ratio * pressure * alpha


def cost(nbytes, flops=0):
    return pl.CostEstimate(flops=flops, bytes_accessed=nbytes, transcendentals=0)


def split_slab(me, parts, after, H, C):
    arrays, steps, N = [], [], 0
    for members, (lv0, lv1), (r0, r1) in parts:
        for a in members:
            if not any(a is seen for seen in arrays):
                arrays.append(a)
            t = [a is seen for seen in arrays].index(True)
            for lv in range(lv0, lv1):
                steps.append((t, lv, r0, r1 - r0, N))
                N += r1 - r0
    nb = arrays[0].shape[1]

    def kernel(me_ref, *refs):
        ins = refs[: len(arrays)]
        outs = refs[len(arrays) + len(after) :][:H]
        stage, sem_in, sem_out = refs[len(arrays) + len(after) + H :]
        core, own = lax.rem(me_ref[0], nb), me_ref[1]
        loads = []
        for n, (t, lv, r0, rows, off) in enumerate(steps):
            loads.append(
                pltpu.make_async_copy(
                    ins[t].at[lv, core, pl.ds(r0, rows), :], stage.at[pl.ds(off, rows), :], sem_in.at[n]
                )
            )
            loads[-1].start()
        stores = []
        for n, (t, lv, r0, rows, off) in enumerate(steps):
            loads[n].wait()
            for m in [*range(1, H), 0]:
                block = lax.bitwise_xor(own, m)
                cols = pl.ds(pl.multiple_of(block * C, C), C)
                stores.append(
                    pltpu.make_async_copy(
                        stage.at[pl.ds(off, rows), cols], outs[m].at[pl.ds(off, rows), :], sem_out.at[n, m]
                    )
                )
                stores[-1].start()
        for c in stores:
            c.wait()

    return pl.pallas_call(
        kernel,
        out_shape=[sds(N, C)] * H,
        in_specs=[SMEM] + [ANY] * (len(arrays) + len(after)),
        out_specs=[ANY] * H,
        scratch_shapes=[
            pltpu.VMEM((N, H * C), f32),
            pltpu.SemaphoreType.DMA((len(steps),)),
            pltpu.SemaphoreType.DMA((len(steps), H)),
        ],
        cost_estimate=cost(8 * N * H * C),
    )(me, *arrays, *after)


def regroup(me, pieces, after, H, nb):
    N, C = pieces[0].shape

    def kernel(me_ref, *refs):
        ins, outs = refs[:H], refs[H + len(after) :][:H]
        stage, sem_in, sem_out = refs[H + len(after) + H :]
        z, j = lax.div(me_ref[0], nb), me_ref[1]
        loads = [
            pltpu.make_async_copy(ins[m], stage.at[lax.bitwise_xor(j, m)], sem_in.at[m]) for m in range(H)
        ]
        for c in loads:
            c.start()
        for c in loads:
            c.wait()
        stores = [
            pltpu.make_async_copy(stage.at[lax.bitwise_xor(z, q)], outs[q], sem_out.at[q])
            for q in far_first(H) + [0]
        ]
        for c in stores:
            c.start()
        for c in stores:
            c.wait()

    return pl.pallas_call(
        kernel,
        out_shape=[sds(N, C)] * H,
        in_specs=[SMEM] + [ANY] * (H + len(after)),
        out_specs=[ANY] * H,
        scratch_shapes=[
            pltpu.VMEM((H, N, C), f32),
            pltpu.SemaphoreType.DMA((H,)),
            pltpu.SemaphoreType.DMA((H,)),
        ],
        cost_estimate=cost(8 * H * N * C),
    )(me, *pieces, *after)


def far_first(H):
    return sorted(range(1, H), key=lambda q: (-q.bit_length(), q))


def moved(x, G, H, ds, dr):
    pairs = [(s * H + r, (s ^ ds) * H + (r ^ dr)) for s in range(G) for r in range(H)]
    return lax.ppermute(x, AXES, pairs)


def coefficients(me, chunks, layout, planes, rims, after, G, H, L, R, C):
    nz = G * L
    wide = -(-nz // 128) * 128
    flat = [p for chunk in chunks for p in chunk]

    def kernel(me_ref, terrain, mass, land, top, rim_t, rim_m, *refs):
        ins = refs[: len(flat)]
        geo, couple, inv, rim, west, east, th, pr, ra, sem = refs[len(flat) + len(after) :]
        i = me_ref[0]
        copies = []
        for c, parts in enumerate(layout):
            for q in range(H):
                src = ins[c * H + q]
                for what, e, lv0, levels, off in parts:
                    s = lax.bitwise_xor(i, q * (G // H) + e)
                    for lv in range(levels):
                        if what == 2:
                            rows, dst = ra.shape[1], ra.at[s]
                        else:
                            rows, dst = R, (th, pr)[what].at[s * L + lv0 + lv]
                        copies.append(
                            pltpu.make_async_copy(
                                src.at[pl.ds(off + lv * R, rows), :], dst, sem.at[len(copies)]
                            )
                        )
                        copies[-1].start()
        for c in copies:
            c.wait()

        run = jnp.zeros((2, C), f32)
        for s in range(G):
            for lv in range(L):
                run = run + ra[s, 2 * lv : 2 * lv + 2, :]
                rim[s * L + lv] = rim_t[...] + rim_m[...] * run / nz

        def rows_step(b, _):
            rows = pl.ds(pl.multiple_of(b * 8, 8), 8)
            ter, mas = terrain[rows, :], mass[rows, :]
            limit = jnp.where(land[rows, :] > 0, top[rows, :], 0)
            alpha, sound = states(th[0, rows, :], pr[0, rows, :])
            run = alpha
            below = jnp.zeros_like(alpha)
            ratio = jnp.zeros_like(alpha)
            lane = lax.broadcasted_iota(jnp.int32, (8, wide), 1)
            first = jnp.zeros((8, wide), f32)
            final = jnp.zeros((8, wide), f32)
            for k in range(nz):
                height = ter + mas * run / nz
                geo[k, rows, :] = height
                first = jnp.where(lane == k, height[:, :1], first)
                final = jnp.where(lane == k, height[:, C - 1 :], final)
                damping = jnp.where(k < limit, 1.0 + land_boost, 1.0).astype(f32)
                if k + 1 < nz:
                    alpha, sound_next = states(th[k + 1, rows, :], pr[k + 1, rows, :])
                    run = run + alpha
                    above = couple_rate * 0.5 * (sound + sound_next)
                    sound = sound_next
                else:
                    above = jnp.zeros_like(below)
                denom = damping + below + above - below * ratio
                rec = 1.0 / denom
                ratio = above * rec
                couple[k, rows, :] = above
                inv[k, rows, :] = rec
                below = above
            west[rows, :] = first
            east[rows, :] = final
            return 0

        lax.fori_loop(0, R // 8, rows_step, 0)

    VM = pl.BlockSpec(memory_space=pltpu.VMEM)
    ncopy = sum(levels for parts in layout for _, _, _, levels, _ in parts) * H
    return pl.pallas_call(
        kernel,
        out_shape=[sds(nz, R, C)] * 3 + [sds(nz, 2, C)] + [sds(R, wide)] * 2,
        in_specs=[SMEM] + [VM] * 6 + [ANY] * (len(flat) + len(after)),
        out_specs=[VM] * 6,
        scratch_shapes=[
            pltpu.VMEM((nz, R, C), f32),
            pltpu.VMEM((nz, R, C), f32),
            pltpu.VMEM((G, max(8, 2 * L), C), f32),
            pltpu.SemaphoreType.DMA((ncopy,)),
        ],
        cost_estimate=cost(24 * nz * R * C, 60 * nz * R * C),
    )(me, *planes, *rims, *flat, *after)


def lifted(me, geo, rim, west, east, after):
    nz, R, C = geo.shape
    deep = 4 if nz % 4 == 0 else 1

    def kernel(me_ref, geo_ref, rim_ref, west_ref, east_ref, *refs):
        out_ref = refs[-1]
        lane = lax.broadcasted_iota(jnp.int32, (R, C), 1)
        row = lax.broadcasted_iota(jnp.int32, (R, C), 0)
        level = lax.broadcasted_iota(jnp.int32, west_ref.shape, 1)
        for d in range(deep):
            here = level == pl.program_id(0) * deep + d
            column = lambda ref: jnp.sum(jnp.where(here, ref[...], 0.0), axis=1, keepdims=True)
            g = geo_ref[d]
            north = jnp.where(row == 0, rim_ref[d, 0:1, :], pltpu.roll(g, 1, 0))
            south = jnp.where(row == R - 1, rim_ref[d, 1:2, :], pltpu.roll(g, R - 1, 0))
            left = jnp.where(lane == 0, column(west_ref), pltpu.roll(g, 1, 1))
            right = jnp.where(lane == C - 1, column(east_ref), pltpu.roll(g, C - 1, 1))
            out_ref[d] = lift_rate * (south + north + right + left - 4.0 * g)

    block = lambda *shape: pl.BlockSpec((deep, *shape), lambda k: (k, 0, 0))
    side = pl.BlockSpec(west.shape, lambda k: (0, 0))
    return [
        pl.pallas_call(
            kernel,
            out_shape=sds(nz, R, C),
            grid=(nz // deep,),
            in_specs=[SMEM, block(R, C), block(2, C), side, side] + [ANY] * len(after),
            out_specs=block(R, C),
            cost_estimate=cost(8 * nz * R * C, 8 * nz * R * C),
        )(me, geo, rim, west, east, *after)
    ]


def smoothed(me, wind, before, behind, after):
    L, RS, Y = wind.shape

    def kernel(me_ref, wind_ref, before_ref, behind_ref, *refs):
        out_ref = refs[-1]
        lane = lax.broadcasted_iota(jnp.int32, (RS, Y), 1)
        row = lax.broadcasted_iota(jnp.int32, (RS, Y), 0)
        w = wind_ref[0]
        north = jnp.where(row == 0, before_ref[0], pltpu.roll(w, 1, 0))
        south = jnp.where(row == RS - 1, behind_ref[0], pltpu.roll(w, RS - 1, 0))
        left = jnp.where(lane == 0, 0.0, pltpu.roll(w, 1, 1))
        right = jnp.where(lane == Y - 1, 0.0, pltpu.roll(w, Y - 1, 1))
        out_ref[0] = w + smooth_rate * (south + north + right + left - 4.0 * w)

    block = lambda rows: pl.BlockSpec((1, rows, Y), lambda k: (k, 0, 0))
    return [
        pl.pallas_call(
            kernel,
            out_shape=sds(L, RS, Y),
            grid=(L,),
            in_specs=[SMEM, block(RS), block(1), block(1)] + [ANY] * len(after),
            out_specs=block(RS),
            cost_estimate=cost(8 * L * RS * Y, 8 * L * RS * Y),
        )(me, wind, before, behind, *after)
    ]


def substitute(me, pieces, lift, couple, inv, wind, r0, rows, G, H, L, R, C):
    nz = G * L
    nb = G // H
    held = [] if wind is None else [wind]

    def kernel(me_ref, lift_ref, couple_ref, inv_ref, *refs):
        ins = refs[:H]
        out, fo, li, co, iv, sem = refs[H + len(held) :]
        i = me_ref[0]
        where = pl.ds(r0, rows)
        copies = [
            pltpu.make_async_copy(lift_ref.at[:, where, :], li, sem.at[G]),
            pltpu.make_async_copy(couple_ref.at[:, where, :], co, sem.at[G + 1]),
            pltpu.make_async_copy(inv_ref.at[:, where, :], iv, sem.at[G + 2]),
        ]
        for k in range(G):
            s = lax.bitwise_xor(i, k)
            copies.append(
                pltpu.make_async_copy(
                    ins[k // nb].at[pl.ds(k % nb * (L * rows), L * rows), :],
                    fo.at[pl.ds(pl.multiple_of(s * (L * rows), 8), L * rows), :],
                    sem.at[k],
                )
            )
        for c in copies:
            c.start()
        for c in copies:
            c.wait()

        def step(b, _):
            base = pl.multiple_of(b * 8, 8)
            part = pl.ds(base, 8)
            value = jnp.zeros((8, C), f32)
            for k in range(nz):
                force = fo[pl.ds(pl.multiple_of(k * rows + base, 8), 8), :] + li[k, part, :]
                if k:
                    force = force + co[k - 1, part, :] * value
                value = force * iv[k, part, :]
                li[k, part, :] = value
            for k in range(nz - 2, -1, -1):
                value = li[k, part, :] + (co[k, part, :] * iv[k, part, :]) * value
                li[k, part, :] = value
            return 0

        lax.fori_loop(0, rows // 8, step, 0)
        done = pltpu.make_async_copy(li, out.at[:, where, :], sem.at[G + 3])
        done.start()
        done.wait()

    return pl.pallas_call(
        kernel,
        out_shape=sds(nz, R, C),
        in_specs=[SMEM] + [ANY] * (3 + H + len(held)),
        out_specs=ANY,
        scratch_shapes=[
            pltpu.VMEM((nz * rows, C), f32),
            pltpu.VMEM((nz, rows, C), f32),
            pltpu.VMEM((nz, rows, C), f32),
            pltpu.VMEM((nz, rows, C), f32),
            pltpu.SemaphoreType.DMA((G + 4,)),
        ],
        input_output_aliases={4 + H: 0} if held else {},
        cost_estimate=cost(20 * nz * rows * C, 8 * nz * rows * C),
    )(me, lift, couple, inv, *pieces, *held)


def on_device(theta, pressure, vertical_wind, terrain, column_mass, land_mask, pbl_top):
    G, H = lax.axis_size("gx"), lax.axis_size("gy")
    nb = G // H
    L, RS, Y = theta.shape
    R, C = RS // nb, Y // H
    s, r = lax.axis_index("gx"), lax.axis_index("gy")
    me = jnp.stack([s, r]).astype(jnp.int32)
    slab = lambda a: a.reshape(a.shape[0], nb, -1, Y)
    after = []

    def step(kernel, *args):
        out = kernel(me, *args)
        after[:] = [out[0]]
        return out

    def send_to(x, ds, dr):
        return moved(x, G, H, ds, dr)

    def beside(x, axis, up):
        n = lax.axis_size(axis)
        pairs = [(i, i + 1) if up else (i + 1, i) for i in range(n - 1)]
        return lax.ppermute(x, axis, pairs)

    def family(a):
        return [slab(a)] + [slab(send_to(a, e, 0)) for e in range(1, nb)]

    def cut(parts):
        pieces = step(split_slab, parts, list(after), H, C)
        return [pieces[0]] + [send_to(pieces[m], 0, m) for m in range(1, H)]

    def send(pieces, behind_of=()):
        pieces = step(regroup, pieces, [*after, *behind_of], H, nb)
        out = [pieces[0]] + [None] * (H - 1)
        for q in far_first(H):
            out[q] = send_to(pieces[q], q * nb, 0)
        return out

    def later(*x):
        return lax.optimization_barrier((*x, *after))[: len(x)]

    full = (0, R)
    first = cut([(family(theta[:1]), (0, 1), full)])

    th = family(later(theta)[0])
    mid_levels = max(1, min(3, L - 1))
    second = cut([(th, (1, mid_levels), full)]) if mid_levels > 1 else None
    sources = later(pressure)
    pr = family(sources[0])
    lead = [send(first)]
    layout = [[(0, e, 0, 1, e * R) for e in range(nb)]]

    half = max(1, L // 2)
    third = cut([(th, (mid_levels, L), full), (pr, (0, half), full)])

    sources = later(theta, pressure, vertical_wind)
    before = beside(jnp.stack([a[:, RS - 1 :] for a in sources]), "gy", True)
    behind = beside(jnp.stack([a[:, :1] for a in sources]), "gy", False)

    if second is not None:
        lead.append(send(second))
        n = mid_levels - 1
        layout.append([(0, e, 1, n, e * n * R) for e in range(nb)])

    blown = step(smoothed, vertical_wind, before[2], behind[2], list(after))[0]
    safe = lambda p: jnp.where(p > 0, p, 1.0)
    theta, pressure, before, behind = later(theta, pressure, before, behind)
    rims = []
    for b in range(nb):
        lines = []
        for lo, src in ((b * R - 1, before), ((b + 1) * R, behind)):
            if 0 <= lo < RS:
                t, p = theta[:, lo, :], pressure[:, lo, :]
            else:
                t, p = src[0, :, 0, :], safe(src[1, :, 0, :])
            lines.append(states(t, p)[0])
        rims.append(jnp.stack(lines, 1).reshape(2 * L, Y))
    tall = -(-2 * L // 8) * 8
    rim = jnp.pad(jnp.stack(rims), ((0, 0), (0, tall - 2 * L), (0, 0))).reshape(1, nb * tall, Y)
    rim, blown = family(rim), family(blown)

    fourth = cut([(pr, (half, L), full), (rim, (0, 1), (0, tall))])
    lead.append(send(third))
    plane_rim = lambda a: jnp.concatenate([beside(a[-1:], "gx", True), beside(a[:1], "gx", False)], 0)
    rim_planes = [plane_rim(a) for a in later(terrain, column_mass)]
    n, base = L - mid_levels, nb * (L - mid_levels) * R
    layout.append(
        [(0, e, mid_levels, n, e * n * R) for e in range(nb)]
        + [(1, e, 0, half, base + e * half * R) for e in range(nb)]
    )
    last = max(8, R // 4 // 8 * 8)
    rows_cut = [(0, R - last), (R - last, R)]
    cuts = [cut([(blown, (0, L), rows_cut[0])])]
    lead.append(send(fourth))
    n = L - half
    layout.append(
        [(1, e, half, n, e * n * R) for e in range(nb)]
        + [(2, e, 0, 1, nb * n * R + e * tall) for e in range(nb)]
    )
    cuts.append(cut([(blown, (0, L), rows_cut[1])]))
    winds = [send(cuts[0], lead[-2][1:])]

    planes = (terrain, column_mass, land_mask, pbl_top)
    geo, couple, inv, rim_geo, west, east = step(
        coefficients, lead, layout, planes, rim_planes, list(after), G, H, L, R, C
    )
    west, east = beside(east, "gy", True), beside(west, "gy", False)
    lift = step(lifted, geo, rim_geo, west, east, list(after))[0]
    winds.append(send(cuts[1]))

    wind = None
    for (r0, r1), pieces in zip(rows_cut, winds):
        wind = substitute(me, pieces, lift, couple, inv, wind, r0, r1 - r0, G, H, L, R, C)
    return wind, geo


def solution(mesh):
    placed = (P("gx", "gy", None),) * 3 + (P("gx", "gy"),) * 4

    fn = jax.shard_map(
        on_device,
        mesh=mesh,
        in_specs=placed,
        out_specs=(P(None, "gx", "gy"), P(None, "gx", "gy")),
        check_vma=False,
    )

    def traced(*args):
        jax.eval_shape(fn, *args)
        return fn(*args)

    return traced
```

time: 547 us -> 378 us (0.69)
  waiting for transfers between devices: 338 us -> 184 us
  Pallas kernels: 0 us -> 85.4 us
  local copies, waits for them, and re-layouts: 94.8 us -> 15.5 us
  other arithmetic: 47.2 us -> 3.41 us
  starting transfers between devices: 63.8 us -> 84.8 us
    all_to_all x6 -> x0, waiting for transfers between devices: 338 us -> none  [the longest x1 78.7 us: on_device(): lax.all_to_all(lax.all_to_all(vertical_wind, 'gy', split_axis=2, concat_a...]
    ppermute x8 -> x49, waiting for transfers between devices: 0.02 us -> 184 us  [the longest x41 174 us: moved(): return lax.ppermute(x, AXES, pairs)]
    pallas_call x0 -> x17, Pallas kernels: none -> 85.4 us  [the longest x6 21.6 us: regroup(): pl.pallas_call(kernel, out_shape=[sds(N, C)] * H, in_specs=[SMEM] + [ANY]...]
    ppermute x8 -> x49, starting transfers between devices: 26.2 us -> 84.8 us  [the longest x41 46.5 us: moved(): return lax.ppermute(x, AXES, pairs)]
    all_to_all x11 -> x0, local copies, waits for them, and re-layouts: 54.9 us -> none  [the longest x3 17.2 us: on_device(): lax.all_to_all(pressure, 'gy', split_axis=2, concat_axis=1, tiled=True)]
    all_to_all x6 -> x0, starting transfers between devices: 37.6 us -> none  [the longest x1 8.04 us: on_device(): lax.all_to_all(lax.all_to_all(vertical_wind, 'gy', split_axis=2, concat_a...]
    add x2 -> x0, other arithmetic: 31.5 us -> none  [the longest x1 24.9 us: on_device(): wind_col + smooth_rate * laplacian(wind_pad)]
    unnamed x40 -> x81, local copies, waits for them, and re-layouts: 19.5 us -> 9.36 us
  transfers between devices with their start and end apart: 14 -> 49, of which waited for: 6 -> 23; matrix products, arithmetic and copies ran while one was open for 18% -> 2% of each run, Pallas kernels for 0% -> 18%
where the time goes in v1:
time: 378 us; the launch traced here: 374 us
  waiting for transfers between devices  184 us (49%)
  Pallas kernels  85.4 us (23%)
  starting transfers between devices  84.8 us (22%)
  local copies, waits for them, and re-layouts  15.5 us (4%)
    ppermute x41, waiting for transfers between devices, moved(): return lax.ppermute(x, AXES, pairs)  174 us
    ppermute x41, starting transfers between devices, moved(): return lax.ppermute(x, AXES, pairs)  46.5 us
    ppermute x8, starting transfers between devices, beside(): return lax.ppermute(x, axis, pairs)  38.3 us
    pallas_call x6, Pallas kernels, regroup(): pl.pallas_call(kernel, out_shape=[sds(N, C)] * H, in_specs=[SMEM] + [ANY]...  21.6 us
    pallas_call x6, Pallas kernels, split_slab(): pl.pallas_call(kernel, out_shape=[sds(N, C)] * H, in_specs=[SMEM] + [ANY]...  19.7 us
    pallas_call x1, Pallas kernels, coefficients(): pl.pallas_call(kernel, out_shape=[sds(nz, R, C)] * 3 + [sds(nz, 2, C)] +...  14.8 us
    pallas_call x2, Pallas kernels, substitute(): pl.pallas_call(kernel, out_shape=sds(nz, R, C), in_specs=[SMEM] + [ANY] *...  13.5 us
    ppermute x8, waiting for transfers between devices, beside(): return lax.ppermute(x, axis, pairs)  10.1 us
  transfers between devices with their start and end apart: 49, of which 23 were waited for; matrix products, arithmetic and copies ran while one was open for 2% of the time, Pallas kernels for 18%

profile of v1, /device:TPU:12, one launch (start us, length us, event | category | flops | bytes accessed | tf_op | source)
XLA Modules:
  0.0 374.3 jit_solution(2019346014302068422)
XLA Ops:
  0.6 1.3 slice.63
  2.8 1.9 collective-permute-done
  5.6 2.8 shard_map.86
  8.6 7.4 %collective-permute-done.1 = f32[4,256,1024]{2,1,0:T(8,128)} collective-permute-done((f32[4,256,1024]{2,1,0:T(8,128)}, f32[4,256,1024]{2,1,0:T(8,128)}, u32[]{:S(2)}, u32[]{:S(2)}) %collective-permute-start.1) | collective-permute-done | bytes 4194336 | tf_op jit(solution)/shard_map/ppermute | solution.py:132
  16.0 3.3 shard_map.87
  19.5 1.5 collective-permute-start.3
  21.5 1.5 collective-permute-start.5
  23.0 1.5 collective-permute-start.11
  24.5 4.2 %collective-permute-done.3.refs_1_ = f32[256,256]{1,0:T(8,128)S(1)} collective-permute-done((f32[256,256]{1,0:T(8,128)S(1)}, f32[256,256]{1,0:T(8,128)S(1)}, u32[]{:S(2)}, u32[]{:S(2)}) %collective-permute-start.3) | collective-permute-done | bytes 262176 | tf_op jit(solution)/shard_map/ppermute | solution.py:132
  29.2 6.6 %collective-permute-done.4.refs_2_ = f32[256,256]{1,0:T(8,128)S(1)} collective-permute-done((f32[256,256]{1,0:T(8,128)S(1)}, f32[256,256]{1,0:T(8,128)S(1)}, u32[]{:S(2)}, u32[]{:S(2)}) %collective-permute-start.4) | collective-permute-done | bytes 262176 | tf_op jit(solution)/shard_map/ppermute | solution.py:132
  37.3 2.9 shard_map.88
  40.2 3.6 shard_map.89
  44.8 1.1 slice_bitcast_fusion.2
  46.1 2.2 collective-permute-start.9
  48.3 4.5 %collective-permute-start.10 = (f32[3,4,1,1024]{3,2,1,0:T(1,128)S(1)}, f32[3,4,1,1024]{3,2,1,0:T(1,128)S(1)}, u32[]{:S(2)}, u32[]{:S(2)}) collective-permute-start(f32[3,4,1,1024]{3,2,1,0:T(1,128)S(1)} %pad_maximum_fusion.1), channel_id=1, source_target_pairs={{1,0},{2,1},{3,2},{5,4},{6,5},{7,6},{9,8},{10,9},{11,10},{13,12},{... | collective-permute-start | bytes 147464 | tf_op jit(solution)/shard_map/ppermute | solution.py:370
  52.9 5.6 %collective-permute-done.12.refs_2_ = f32[512,256]{1,0:T(8,128)S(1)} collective-permute-done((f32[512,256]{1,0:T(8,128)}, f32[512,256]{1,0:T(8,128)S(1)}, u32[]{:S(2)}, u32[]{:S(2)}) %collective-permute-start.12) | collective-permute-done | bytes 524320 | tf_op jit(solution)/shard_map/ppermute | solution.py:132
  60.1 3.6 shard_map.90
  65.0 6.4 %shard_map.91.refs_4_ = f32[4,256,1024]{2,1,0:T(8,128)} custom-call(s32[2]{0:T(128)} %pad_add_fusion.me_ref, f32[4,256,1024]{2,1,0:T(8,128)} %wind_ref.1, f32[4,1,1024]{2,1,0:T(1,128)} %slice_bitcast_fusion.1.before_ref, f32[4,1,1024]{2,1,0:T(1,128)} %slice_bitcast_fusion.behind_ref, f32[512,256]{1,0:T(8,128)} %get-tuple-element.85.refs_0_.refs_4_), custom_call_target="tpu_custom_call" | custom-call | flops 8388608 | bytes 8388608 | tf_op jit(solution)/shard_map/pallas_call | solution.py:272
  72.0 2.6 collective-permute-start.20
  75.0 1.2 exponential_multiply_fusion
  76.4 6.9 %collective-permute-done.19.refs_1_ = f32[256,256]{1,0:T(8,128)S(1)} collective-permute-done((f32[256,256]{1,0:T(8,128)S(1)}, f32[256,256]{1,0:T(8,128)S(1)}, u32[]{:S(2)}, u32[]{:S(2)}) %collective-permute-start.19) | collective-permute-done | bytes 262176 | tf_op jit(solution)/shard_map/ppermute | solution.py:132
  83.3 9.2 %collective-permute-done.20.refs_2_ = f32[256,256]{1,0:T(8,128)S(1)} collective-permute-done((f32[256,256]{1,0:T(8,128)S(1)}, f32[256,256]{1,0:T(8,128)S(1)}, u32[]{:S(2)}, u32[]{:S(2)}) %collective-permute-start.20) | collective-permute-done | bytes 262176 | tf_op jit(solution)/shard_map/ppermute | solution.py:132
  93.4 4.9 %collective-permute-done.21.refs_3_ = f32[256,256]{1,0:T(8,128)S(1)} collective-permute-done((f32[256,256]{1,0:T(8,128)}, f32[256,256]{1,0:T(8,128)S(1)}, u32[]{:S(2)}, u32[]{:S(2)}) %collective-permute-start.21) | collective-permute-done | bytes 262176 | tf_op jit(solution)/shard_map/ppermute | solution.py:132
  98.3 1.3 collective-permute-done.14
  99.5 3.0 collective-permute-start.23
  102.6 3.3 shard_map.92
  105.9 13.3 %collective-permute-done.7.refs_2_ = f32[768,256]{1,0:T(8,128)S(1)} collective-permute-done((f32[768,256]{1,0:T(8,128)S(1)}, f32[768,256]{1,0:T(8,128)S(1)}, u32[]{:S(2)}, u32[]{:S(2)}) %collective-permute-start.7) | collective-permute-done | bytes 786464 | tf_op jit(solution)/shard_map/ppermute | solution.py:132
  120.3 4.3 %shard_map.93 = (f32[768,256]{1,0:T(8,128)}, f32[768,256]{1,0:T(8,128)}, f32[768,256]{1,0:T(8,128)}, f32[768,256]{1,0:T(8,128)}) custom-call(s32[2]{0:T(128)} %pad_add_fusion.me_ref, f32[768,256]{1,0:T(8,128)} %get-tuple-element.75.refs_4_.refs_0_, f32[768,256]{1,0:T(8,128)} %copy-done.8, f32[768,256]{1,0:T(8,128)} %copy-done.10, f32[768,256]{1,0:T(8,128)} %copy-done.11, ...), custom_call_target="tpu_custom_call" | custom-call | bytes 6291456 | tf_op jit(solution)/shard_map/pallas_call | solution.py:112
  124.6 2.5 collective-permute-start.25
  127.2 2.4 collective-permute-start.30
  129.5 1.4 collective-permute-start.26
  131.0 3.7 shard_map.94
  134.7 1.8 collective-permute-start.27
  137.3 8.9 %collective-permute-start.35 = (f32[768,256]{1,0:T(8,128)}, f32[768,256]{1,0:T(8,128)S(1)}, u32[]{:S(2)}, u32[]{:S(2)}) collective-permute-start(f32[768,256]{1,0:T(8,128)} %get-tuple-element.111), channel_id=1, source_target_pairs={{0,1},{1,0},{2,3},{3,2},{4,5},{5,4},{6,7},{7,6},{8,9},{9,8},{10,11... | collective-permute-start | bytes 2359304 | tf_op jit(solution)/shard_map/ppermute | solution.py:132
  146.2 1.5 collective-permute-start.36
  147.7 10.1 %collective-permute-done.25.refs_5_.refs_9_ = f32[768,256]{1,0:T(8,128)S(1)} collective-permute-done((f32[768,256]{1,0:T(8,128)}, f32[768,256]{1,0:T(8,128)S(1)}, u32[]{:S(2)}, u32[]{:S(2)}) %collective-permute-start.25) | collective-permute-done | bytes 786464 | tf_op jit(solution)/shard_map/ppermute | solution.py:132
  157.8 2.3 collective-permute-start.37
  160.2 28.4 %collective-permute-done.26.refs_6_.refs_10_ = f32[768,256]{1,0:T(8,128)S(1)} collective-permute-done((f32[768,256]{1,0:T(8,128)}, f32[768,256]{1,0:T(8,128)S(1)}, u32[]{:S(2)}, u32[]{:S(2)}) %collective-permute-start.26) | collective-permute-done | bytes 786464 | tf_op jit(solution)/shard_map/ppermute | solution.py:132
  189.0 3.7 shard_map.95
  192.7 19.2 %collective-permute-done.27.refs_7_.refs_11_ = f32[768,256]{1,0:T(8,128)S(1)} collective-permute-done((f32[768,256]{1,0:T(8,128)}, f32[768,256]{1,0:T(8,128)S(1)}, u32[]{:S(2)}, u32[]{:S(2)}) %collective-permute-start.27) | collective-permute-done | bytes 786464 | tf_op jit(solution)/shard_map/ppermute | solution.py:132
  211.9 3.0 collective-permute-start.33
  216.1 1.9 collective-permute-start.17
  218.0 3.0 shard_map.96
  221.1 4.3 %shard_map.97 = (f32[768,256]{1,0:T(8,128)}, f32[768,256]{1,0:T(8,128)}, f32[768,256]{1,0:T(8,128)}, f32[768,256]{1,0:T(8,128)}) custom-call(s32[2]{0:T(128)} %pad_add_fusion.me_ref, f32[768,256]{1,0:T(8,128)} %get-tuple-element.106.refs_4_.refs_0_, f32[768,256]{1,0:T(8,128)} %copy-done.9, f32[768,256]{1,0:T(8,128)} %collective-permute-done.36.refs_2_, ...), custom_call_target="tpu_custom_call" | custom-call | bytes 6291456 | tf_op jit(solution)/shard_map/pallas_call | solution.py:112
  225.3 21.0 %collective-permute-done.24.refs_7_ = f32[512,256]{1,0:T(8,128)} collective-permute-done((f32[512,256]{1,0:T(8,128)}, f32[512,256]{1,0:T(8,128)}, u32[]{:S(2)}, u32[]{:S(2)}) %collective-permute-start.24) | collective-permute-done | bytes 524320 | tf_op jit(solution)/shard_map/ppermute | solution.py:132
  246.4 1.9 collective-permute-start.18
  249.6 19.1 %collective-permute-start.15 = (f32[1,256]{1,0:T(1,128)S(1)}, f32[1,256]{1,0:T(1,128)S(1)}, u32[]{:S(2)}, u32[]{:S(2)}) collective-permute-start(f32[1,256]{1,0:T(1,128)S(1)} %get-tuple-element.142), channel_id=1, source_target_pairs={{0,4},{4,8},{8,12},{12,16},{16,20},{20,24},{24,28},{1,5},{5,9},{9,... | collective-permute-start | bytes 3080 | tf_op jit(solution)/shard_map/ppermute | solution.py:370
  268.6 5.5 %collective-permute-done.15 = f32[1,256]{1,0:T(1,128)S(1)} collective-permute-done((f32[1,256]{1,0:T(1,128)S(1)}, f32[1,256]{1,0:T(1,128)S(1)}, u32[]{:S(2)}, u32[]{:S(2)}) %collective-permute-start.15) | collective-permute-done | bytes 1056 | tf_op jit(solution)/shard_map/ppermute | solution.py:370
  274.1 1.9 collective-permute-start.16
  276.0 1.3 collective-permute-done.16
  279.7 14.8 %shard_map.98 = (f32[32,128,256]{2,1,0:T(8,128)}, f32[32,128,256]{2,1,0:T(8,128)}, f32[32,128,256]{2,1,0:T(8,128)}, f32[32,2,256]{2,1,0:T(2,128)}, f32[128,128]{1,0:T(8,128)}, /*index=5*/f32[128,128]{1,0:T(8,128)}) custom-call(s32[2]{0:T(128)} %pad_add_fusion.me_ref, f32[128,256]{1,0:T(8,128)} %terrain.1, f32[128,256]{1,0:T(8,128)} %mass.1, ...), custom_call_target="tpu_custom_call" | custom-call | flops 62914560 | bytes 25165824 | tf_op jit(solution)/shard_map/pallas_call | solution.py:208
  294.6 3.3 collective-permute-start.38
  297.9 3.5 collective-permute-start.39
  301.9 2.4 collective-permute-done.39.east_ref
  304.3 2.5 collective-permute-start.42
  306.7 9.3 %shard_map.99.refs_4_.lift_ref = f32[32,128,256]{2,1,0:T(8,128)} custom-call(s32[2]{0:T(128)} %pad_add_fusion.me_ref, f32[32,128,256]{2,1,0:T(8,128)} %get-tuple-element.66.geo_ref.refs_0_, f32[32,2,256]{2,1,0:T(2,128)} %get-tuple-element.117.rim_ref, f32[128,128]{1,0:T(8,128)} %copy-done.30, f32[128,128]{1,0:T(8,128)} %copy-done.32, ...), custom_call_target="tpu_custom_call" | custom-call | flops 8388608 | bytes 8388608 | tf_op jit(solution)/shard_map/pallas_call | solution.py:245
  318.1 2.9 shard_map.100
  321.0 3.3 collective-permute-start.43
  324.3 1.5 collective-permute-start.45
  325.9 4.5 %collective-permute-done.47.refs_2_ = f32[768,256]{1,0:T(8,128)S(1)} collective-permute-done((f32[768,256]{1,0:T(8,128)}, f32[768,256]{1,0:T(8,128)S(1)}, u32[]{:S(2)}, u32[]{:S(2)}) %collective-permute-start.47) | collective-permute-done | bytes 786464 | tf_op jit(solution)/shard_map/ppermute | solution.py:132
  330.3 27.5 %collective-permute-done.48.refs_3_ = f32[768,256]{1,0:T(8,128)S(1)} collective-permute-done((f32[768,256]{1,0:T(8,128)}, f32[768,256]{1,0:T(8,128)S(1)}, u32[]{:S(2)}, u32[]{:S(2)}) %collective-permute-start.48) | collective-permute-done | bytes 786464 | tf_op jit(solution)/shard_map/ppermute | solution.py:132
  358.7 9.0 %shard_map.101.refs_4_ = f32[32,128,256]{2,1,0:T(8,128)} custom-call(s32[2]{0:T(128)} %pad_add_fusion.me_ref, f32[32,128,256]{2,1,0:T(8,128)} %shard_map.99.refs_4_.lift_ref, f32[32,128,256]{2,1,0:T(8,128)} %get-tuple-element.120.couple_ref, f32[32,128,256]{2,1,0:T(8,128)} %get-tuple-element.121.inv_ref, f32[768,256]{1,0:T(8,128)} %get-tuple-element.115.refs_16_.refs_0_, ...), custom_call_target="tpu_custom_call" | custom-call | flops 6291456 | bytes 15728640 | tf_op jit(solution)/shard_map/pallas_call | solution.py:332
  367.7 1.3 collective-permute-done.45.refs_3_
  369.7 4.5 %shard_map.102 = f32[32,128,256]{2,1,0:T(8,128)} custom-call(s32[2]{0:T(128)} %pad_add_fusion.me_ref, f32[32,128,256]{2,1,0:T(8,128)} %shard_map.99.refs_4_.lift_ref, f32[32,128,256]{2,1,0:T(8,128)} %get-tuple-element.120.couple_ref, f32[32,128,256]{2,1,0:T(8,128)} %get-tuple-element.121.inv_ref, ...), custom_call_target="tpu_custom_call", output_to_operand_aliasing={{}: (8, {})} | custom-call | flops 2097152 | bytes 5242880 | tf_op jit(solution)/shard_map/pallas_call | solution.py:332
  (152 shorter events, 22.2 us)
Async XLA Ops:
  1.9 2.7 collective-permute-start
  8.4 7.6 %collective-permute-start.1 = (f32[4,256,1024]{2,1,0:T(8,128)}, f32[4,256,1024]{2,1,0:T(8,128)}, u32[]{:S(2)}, u32[]{:S(2)}) collective-permute-start(f32[4,256,1024]{2,1,0:T(8,128)} %param.7), channel_id=1, source_target_pairs={{0,4},{1,5},{2,6},{3,7},{4,0},{5,1},{6,2},{7,3},{8,12},{9,13},{10,... | collective-permute-start | bytes 12582920 | tf_op jit(solution)/shard_map/ppermute | solution.py:132
  19.3 20.9 %collective-permute-start.2 = (f32[4,256,1024]{2,1,0:T(8,128)}, f32[4,256,1024]{2,1,0:T(8,128)}, u32[]{:S(2)}, u32[]{:S(2)}) collective-permute-start(f32[4,256,1024]{2,1,0:T(8,128)} %param.8), channel_id=1, source_target_pairs={{0,4},{1,5},{2,6},{3,7},{4,0},{5,1},{6,2},{7,3},{8,12},{9,13},{10,... | collective-permute-start | bytes 12582920 | tf_op jit(solution)/shard_map/ppermute | solution.py:132
  19.5 9.2 %collective-permute-start.3 = (f32[256,256]{1,0:T(8,128)S(1)}, f32[256,256]{1,0:T(8,128)S(1)}, u32[]{:S(2)}, u32[]{:S(2)}) collective-permute-start(f32[256,256]{1,0:T(8,128)S(1)} %copy-done.39), channel_id=1, source_target_pairs={{0,1},{1,0},{2,3},{3,2},{4,5},{5,4},{6,7},{7,6},{8,9},{9,8},{10,11... | collective-permute-start | bytes 786440 | tf_op jit(solution)/shard_map/ppermute | solution.py:132
  21.0 14.8 %collective-permute-start.4 = (f32[256,256]{1,0:T(8,128)S(1)}, f32[256,256]{1,0:T(8,128)S(1)}, u32[]{:S(2)}, u32[]{:S(2)}) collective-permute-start(f32[256,256]{1,0:T(8,128)S(1)} %copy-done.38), channel_id=1, source_target_pairs={{0,2},{1,3},{2,0},{3,1},{4,6},{5,7},{6,4},{7,5},{8,10},{9,11},{10,... | collective-permute-start | bytes 786440 | tf_op jit(solution)/shard_map/ppermute | solution.py:132
  21.5 14.3 %collective-permute-start.5 = (f32[256,256]{1,0:T(8,128)S(1)}, f32[256,256]{1,0:T(8,128)S(1)}, u32[]{:S(2)}, u32[]{:S(2)}) collective-permute-start(f32[256,256]{1,0:T(8,128)S(1)} %copy-done.37), channel_id=1, source_target_pairs={{0,3},{1,2},{2,1},{3,0},{4,7},{5,6},{6,5},{7,4},{8,11},{9,10},{10,... | collective-permute-start | bytes 786440 | tf_op jit(solution)/shard_map/ppermute | solution.py:132
  23.0 29.8 %collective-permute-start.11 = (f32[512,256]{1,0:T(8,128)}, f32[512,256]{1,0:T(8,128)S(1)}, u32[]{:S(2)}, u32[]{:S(2)}) collective-permute-start(f32[512,256]{1,0:T(8,128)} %get-tuple-element.82), channel_id=1, source_target_pairs={{0,1},{1,0},{2,3},{3,2},{4,5},{5,4},{6,7},{7,6},{8,9},{9,8},{10,11... | collective-permute-start | bytes 1572872 | tf_op jit(solution)/shard_map/ppermute | solution.py:132
  28.7 7.1 %copy-start.23 = (f32[256,256]{1,0:T(8,128)}, f32[256,256]{1,0:T(8,128)S(1)}, u32[]{:S(2)}) copy-start(f32[256,256]{1,0:T(8,128)S(1)} %collective-permute-done.3.refs_1_) | copy-start | bytes 786436
  28.7 29.8 %collective-permute-start.12 = (f32[512,256]{1,0:T(8,128)}, f32[512,256]{1,0:T(8,128)S(1)}, u32[]{:S(2)}, u32[]{:S(2)}) collective-permute-start(f32[512,256]{1,0:T(8,128)} %get-tuple-element.83), channel_id=1, source_target_pairs={{0,2},{1,3},{2,0},{3,1},{4,6},{5,7},{6,4},{7,5},{8,10},{9,11},{10,... | collective-permute-start | bytes 1572872 | tf_op jit(solution)/shard_map/ppermute | solution.py:132
  35.8 22.7 %collective-permute-start.13 = (f32[512,256]{1,0:T(8,128)}, f32[512,256]{1,0:T(8,128)S(1)}, u32[]{:S(2)}, u32[]{:S(2)}) collective-permute-start(f32[512,256]{1,0:T(8,128)} %get-tuple-element.84), channel_id=1, source_target_pairs={{0,3},{1,2},{2,1},{3,0},{4,7},{5,6},{6,5},{7,4},{8,11},{9,10},{10,... | collective-permute-start | bytes 1572872 | tf_op jit(solution)/shard_map/ppermute | solution.py:132
  46.1 17.7 %collective-permute-start.9 = (f32[3,4,1,1024]{3,2,1,0:T(1,128)S(1)}, f32[3,4,1,1024]{3,2,1,0:T(1,128)S(1)}, u32[]{:S(2)}, u32[]{:S(2)}) collective-permute-start(f32[3,4,1,1024]{3,2,1,0:T(1,128)S(1)} %pad_maximum_fusion), channel_id=1, source_target_pairs={{0,1},{1,2},{2,3},{4,5},{5,6},{6,7},{8,9},{9,10},{10,11},{12,13},{... | collective-permute-start | bytes 147464 | tf_op jit(solution)/shard_map/ppermute | solution.py:370
  48.3 16.0 %collective-permute-start.10 = (f32[3,4,1,1024]{3,2,1,0:T(1,128)S(1)}, f32[3,4,1,1024]{3,2,1,0:T(1,128)S(1)}, u32[]{:S(2)}, u32[]{:S(2)}) collective-permute-start(f32[3,4,1,1024]{3,2,1,0:T(1,128)S(1)} %pad_maximum_fusion.1), channel_id=1, source_target_pairs={{1,0},{2,1},{3,2},{5,4},{6,5},{7,6},{9,8},{10,9},{11,10},{13,12},{... | collective-permute-start | bytes 147464 | tf_op jit(solution)/shard_map/ppermute | solution.py:370
  65.0 6.5 %copy-start.36 = (f32[256,256]{1,0:T(8,128)S(1)}, f32[256,256]{1,0:T(8,128)}, u32[]{:S(2)}) copy-start(f32[256,256]{1,0:T(8,128)} %get-tuple-element.94) | copy-start | bytes 786436
  65.0 7.0 %copy-start.35 = (f32[256,256]{1,0:T(8,128)S(1)}, f32[256,256]{1,0:T(8,128)}, u32[]{:S(2)}) copy-start(f32[256,256]{1,0:T(8,128)} %get-tuple-element.95) | copy-start | bytes 786436
  65.0 18.3 %copy-start.33 = (f32[768,256]{1,0:T(8,128)S(1)}, f32[768,256]{1,0:T(8,128)}, u32[]{:S(2)}) copy-start(f32[768,256]{1,0:T(8,128)} %get-tuple-element.77) | copy-start | bytes 2359300
  71.5 58.1 %collective-permute-start.31 = (f32[4,256,1024]{2,1,0:T(8,128)}, f32[4,256,1024]{2,1,0:T(8,128)}, u32[]{:S(2)}, u32[]{:S(2)}) collective-permute-start(f32[4,256,1024]{2,1,0:T(8,128)} %shard_map.91.refs_4_), channel_id=1, source_target_pairs={{0,4},{1,5},{2,6},{3,7},{4,0},{5,1},{6,2},{7,3},{8,12},{9,13},{10,... | collective-permute-start | bytes 12582920 | tf_op jit(solution)/shard_map/ppermute | solution.py:132
  71.5 11.8 %collective-permute-start.19 = (f32[256,256]{1,0:T(8,128)S(1)}, f32[256,256]{1,0:T(8,128)S(1)}, u32[]{:S(2)}, u32[]{:S(2)}) collective-permute-start(f32[256,256]{1,0:T(8,128)S(1)} %copy-done.36), channel_id=1, source_target_pairs={{0,8},{1,9},{2,10},{3,11},{4,12},{5,13},{6,14},{7,15},{8,0},{9,1},... | collective-permute-start | bytes 786440 | tf_op jit(solution)/shard_map/ppermute | solution.py:132
  72.0 20.6 %collective-permute-start.20 = (f32[256,256]{1,0:T(8,128)S(1)}, f32[256,256]{1,0:T(8,128)S(1)}, u32[]{:S(2)}, u32[]{:S(2)}) collective-permute-start(f32[256,256]{1,0:T(8,128)S(1)} %copy-done.35), channel_id=1, source_target_pairs={{0,16},{1,17},{2,18},{3,19},{4,20},{5,21},{6,22},{7,23},{8,24},{9,... | collective-permute-start | bytes 786440 | tf_op jit(solution)/shard_map/ppermute | solution.py:132
  74.6 23.7 %collective-permute-start.21 = (f32[256,256]{1,0:T(8,128)}, f32[256,256]{1,0:T(8,128)S(1)}, u32[]{:S(2)}, u32[]{:S(2)}) collective-permute-start(f32[256,256]{1,0:T(8,128)} %get-tuple-element.96), channel_id=1, source_target_pairs={{0,24},{1,25},{2,26},{3,27},{4,28},{5,29},{6,30},{7,31},{8,16},{9,... | collective-permute-start | bytes 786440 | tf_op jit(solution)/shard_map/ppermute | solution.py:132
  75.0 24.5 %collective-permute-start.6 = (f32[768,256]{1,0:T(8,128)}, f32[768,256]{1,0:T(8,128)S(1)}, u32[]{:S(2)}, u32[]{:S(2)}) collective-permute-start(f32[768,256]{1,0:T(8,128)} %get-tuple-element.76), channel_id=1, source_target_pairs={{0,1},{1,0},{2,3},{3,2},{4,5},{5,4},{6,7},{7,6},{8,9},{9,8},{10,11... | collective-permute-start | bytes 2359304 | tf_op jit(solution)/shard_map/ppermute | solution.py:132
  83.3 9.2 %copy-start.20 = (f32[256,256]{1,0:T(8,128)}, f32[256,256]{1,0:T(8,128)S(1)}, u32[]{:S(2)}) copy-start(f32[256,256]{1,0:T(8,128)S(1)} %collective-permute-done.19.refs_1_) | copy-start | bytes 786436
  83.3 35.9 %collective-permute-start.7 = (f32[768,256]{1,0:T(8,128)S(1)}, f32[768,256]{1,0:T(8,128)S(1)}, u32[]{:S(2)}, u32[]{:S(2)}) collective-permute-start(f32[768,256]{1,0:T(8,128)S(1)} %copy-done.33), channel_id=1, source_target_pairs={{0,2},{1,3},{2,0},{3,1},{4,6},{5,7},{6,4},{7,5},{8,10},{9,11},{10,... | collective-permute-start | bytes 2359304 | tf_op jit(solution)/shard_map/ppermute | solution.py:132
  93.3 25.9 %collective-permute-start.8 = (f32[768,256]{1,0:T(8,128)}, f32[768,256]{1,0:T(8,128)S(1)}, u32[]{:S(2)}, u32[]{:S(2)}) collective-permute-start(f32[768,256]{1,0:T(8,128)} %get-tuple-element.78), channel_id=1, source_target_pairs={{0,3},{1,2},{2,1},{3,0},{4,7},{5,6},{6,5},{7,4},{8,11},{9,10},{10,... | collective-permute-start | bytes 2359304 | tf_op jit(solution)/shard_map/ppermute | solution.py:132
  93.4 9.2 %copy-start.29 = (f32[2,8,1024]{2,1,0:T(8,128)}, f32[2,8,1024]{2,1,0:T(8,128)S(1)}, u32[]{:S(2)}) copy-start(f32[2,8,1024]{2,1,0:T(8,128)S(1)} %constant_dynamic-update-slice_fusion) | copy-start | bytes 196612
  98.3 7.6 %copy-start.22 = (f32[256,256]{1,0:T(8,128)}, f32[256,256]{1,0:T(8,128)S(1)}, u32[]{:S(2)}) copy-start(f32[256,256]{1,0:T(8,128)S(1)} %collective-permute-done.21.refs_3_) | copy-start | bytes 786436
  98.3 1.3 collective-permute-start.14
  99.5 25.1 %collective-permute-start.22 = (f32[512,256]{1,0:T(8,128)}, f32[512,256]{1,0:T(8,128)}, u32[]{:S(2)}, u32[]{:S(2)}) collective-permute-start(f32[512,256]{1,0:T(8,128)} %get-tuple-element.97), channel_id=1, source_target_pairs={{0,8},{1,9},{2,10},{3,11},{4,12},{5,13},{6,14},{7,15},{8,0},{9,1},... | collective-permute-start | bytes 1572872 | tf_op jit(solution)/shard_map/ppermute | solution.py:132
  99.5 27.6 %collective-permute-start.23 = (f32[512,256]{1,0:T(8,128)}, f32[512,256]{1,0:T(8,128)}, u32[]{:S(2)}, u32[]{:S(2)}) collective-permute-start(f32[512,256]{1,0:T(8,128)} %get-tuple-element.98), channel_id=1, source_target_pairs={{0,16},{1,17},{2,18},{3,19},{4,20},{5,21},{6,22},{7,23},{8,24},{9,... | collective-permute-start | bytes 1572872 | tf_op jit(solution)/shard_map/ppermute | solution.py:132
  119.2 15.4 %collective-permute-start.28 = (f32[528,256]{1,0:T(8,128)}, f32[528,256]{1,0:T(8,128)S(1)}, u32[]{:S(2)}, u32[]{:S(2)}) collective-permute-start(f32[528,256]{1,0:T(8,128)} %get-tuple-element.103), channel_id=1, source_target_pairs={{0,1},{1,0},{2,3},{3,2},{4,5},{5,4},{6,7},{7,6},{8,9},{9,8},{10,11... | collective-permute-start | bytes 1622024 | tf_op jit(solution)/shard_map/ppermute | solution.py:132
  119.2 17.3 %collective-permute-start.29 = (f32[528,256]{1,0:T(8,128)}, f32[528,256]{1,0:T(8,128)S(1)}, u32[]{:S(2)}, u32[]{:S(2)}) collective-permute-start(f32[528,256]{1,0:T(8,128)} %get-tuple-element.104), channel_id=1, source_target_pairs={{0,2},{1,3},{2,0},{3,1},{4,6},{5,7},{6,4},{7,5},{8,10},{9,11},{10,... | collective-permute-start | bytes 1622024 | tf_op jit(solution)/shard_map/ppermute | solution.py:132
  124.6 33.2 %collective-permute-start.25 = (f32[768,256]{1,0:T(8,128)}, f32[768,256]{1,0:T(8,128)S(1)}, u32[]{:S(2)}, u32[]{:S(2)}) collective-permute-start(f32[768,256]{1,0:T(8,128)} %get-tuple-element.100), channel_id=1, source_target_pairs={{0,8},{1,9},{2,10},{3,11},{4,12},{5,13},{6,14},{7,15},{8,0},{9,1},... | collective-permute-start | bytes 2359304 | tf_op jit(solution)/shard_map/ppermute | solution.py:132
  127.2 19.1 %collective-permute-start.30 = (f32[528,256]{1,0:T(8,128)}, f32[528,256]{1,0:T(8,128)}, u32[]{:S(2)}, u32[]{:S(2)}) collective-permute-start(f32[528,256]{1,0:T(8,128)} %get-tuple-element.105), channel_id=1, source_target_pairs={{0,3},{1,2},{2,1},{3,0},{4,7},{5,6},{6,5},{7,4},{8,11},{9,10},{10,... | collective-permute-start | bytes 1622024 | tf_op jit(solution)/shard_map/ppermute | solution.py:132
  129.5 59.0 %collective-permute-start.26 = (f32[768,256]{1,0:T(8,128)}, f32[768,256]{1,0:T(8,128)S(1)}, u32[]{:S(2)}, u32[]{:S(2)}) collective-permute-start(f32[768,256]{1,0:T(8,128)} %get-tuple-element.101), channel_id=1, source_target_pairs={{0,16},{1,17},{2,18},{3,19},{4,20},{5,21},{6,22},{7,23},{8,24},{9,... | collective-permute-start | bytes 2359304 | tf_op jit(solution)/shard_map/ppermute | solution.py:132
  134.7 77.2 %collective-permute-start.27 = (f32[768,256]{1,0:T(8,128)}, f32[768,256]{1,0:T(8,128)S(1)}, u32[]{:S(2)}, u32[]{:S(2)}) collective-permute-start(f32[768,256]{1,0:T(8,128)} %get-tuple-element.102), channel_id=1, source_target_pairs={{0,24},{1,25},{2,26},{3,27},{4,28},{5,29},{6,30},{7,31},{8,16},{9,... | collective-permute-start | bytes 2359304 | tf_op jit(solution)/shard_map/ppermute | solution.py:132
  137.3 74.6 %collective-permute-start.35 = (f32[768,256]{1,0:T(8,128)}, f32[768,256]{1,0:T(8,128)S(1)}, u32[]{:S(2)}, u32[]{:S(2)}) collective-permute-start(f32[768,256]{1,0:T(8,128)} %get-tuple-element.111), channel_id=1, source_target_pairs={{0,1},{1,0},{2,3},{3,2},{4,5},{5,4},{6,7},{7,6},{8,9},{9,8},{10,11... | collective-permute-start | bytes 2359304 | tf_op jit(solution)/shard_map/ppermute | solution.py:132
  146.2 68.6 %collective-permute-start.36 = (f32[768,256]{1,0:T(8,128)}, f32[768,256]{1,0:T(8,128)}, u32[]{:S(2)}, u32[]{:S(2)}) collective-permute-start(f32[768,256]{1,0:T(8,128)} %get-tuple-element.112), channel_id=1, source_target_pairs={{0,2},{1,3},{2,0},{3,1},{4,6},{5,7},{6,4},{7,5},{8,10},{9,11},{10,... | collective-permute-start | bytes 2359304 | tf_op jit(solution)/shard_map/ppermute | solution.py:132
  157.8 63.2 %copy-start.1 = (f32[768,256]{1,0:T(8,128)}, f32[768,256]{1,0:T(8,128)S(1)}, u32[]{:S(2)}) copy-start(f32[768,256]{1,0:T(8,128)S(1)} %collective-permute-done.25.refs_5_.refs_9_) | copy-start | bytes 2359300
  157.8 58.3 %collective-permute-start.37 = (f32[768,256]{1,0:T(8,128)}, f32[768,256]{1,0:T(8,128)}, u32[]{:S(2)}, u32[]{:S(2)}) collective-permute-start(f32[768,256]{1,0:T(8,128)} %get-tuple-element.113), channel_id=1, source_target_pairs={{0,3},{1,2},{2,1},{3,0},{4,7},{5,6},{6,5},{7,4},{8,11},{9,10},{10,... | collective-permute-start | bytes 2359304 | tf_op jit(solution)/shard_map/ppermute | solution.py:132
  188.6 32.5 %copy-start.2 = (f32[768,256]{1,0:T(8,128)}, f32[768,256]{1,0:T(8,128)S(1)}, u32[]{:S(2)}) copy-start(f32[768,256]{1,0:T(8,128)S(1)} %collective-permute-done.26.refs_6_.refs_10_) | copy-start | bytes 2359300
  188.6 57.8 %collective-permute-start.24 = (f32[512,256]{1,0:T(8,128)}, f32[512,256]{1,0:T(8,128)}, u32[]{:S(2)}, u32[]{:S(2)}) collective-permute-start(f32[512,256]{1,0:T(8,128)} %get-tuple-element.99), channel_id=1, source_target_pairs={{0,24},{1,25},{2,26},{3,27},{4,28},{5,29},{6,30},{7,31},{8,16},{9,... | collective-permute-start | bytes 1572872 | tf_op jit(solution)/shard_map/ppermute | solution.py:132
  211.9 9.2 %copy-start.3 = (f32[768,256]{1,0:T(8,128)}, f32[768,256]{1,0:T(8,128)S(1)}, u32[]{:S(2)}) copy-start(f32[768,256]{1,0:T(8,128)S(1)} %collective-permute-done.27.refs_7_.refs_11_) | copy-start | bytes 2359300
  211.9 66.1 %collective-permute-start.32 = (f32[528,256]{1,0:T(8,128)}, f32[528,256]{1,0:T(8,128)}, u32[]{:S(2)}, u32[]{:S(2)}) collective-permute-start(f32[528,256]{1,0:T(8,128)} %get-tuple-element.108), channel_id=1, source_target_pairs={{0,8},{1,9},{2,10},{3,11},{4,12},{5,13},{6,14},{7,15},{8,0},{9,1},... | collective-permute-start | bytes 1622024 | tf_op jit(solution)/shard_map/ppermute | solution.py:132
  211.9 9.2 %copy-start.9 = (f32[768,256]{1,0:T(8,128)}, f32[768,256]{1,0:T(8,128)S(1)}, u32[]{:S(2)}) copy-start(f32[768,256]{1,0:T(8,128)S(1)} %collective-permute-done.35.refs_1_) | copy-start | bytes 2359300
  211.9 66.1 %collective-permute-start.33 = (f32[528,256]{1,0:T(8,128)}, f32[528,256]{1,0:T(8,128)}, u32[]{:S(2)}, u32[]{:S(2)}) collective-permute-start(f32[528,256]{1,0:T(8,128)} %get-tuple-element.109), channel_id=1, source_target_pairs={{0,16},{1,17},{2,18},{3,19},{4,20},{5,21},{6,22},{7,23},{8,24},{9,... | collective-permute-start | bytes 1622024 | tf_op jit(solution)/shard_map/ppermute | solution.py:132
  214.9 64.9 %collective-permute-start.34 = (f32[528,256]{1,0:T(8,128)}, f32[528,256]{1,0:T(8,128)}, u32[]{:S(2)}, u32[]{:S(2)}) collective-permute-start(f32[528,256]{1,0:T(8,128)} %get-tuple-element.110), channel_id=1, source_target_pairs={{0,24},{1,25},{2,26},{3,27},{4,28},{5,29},{6,30},{7,31},{8,16},{9,... | collective-permute-start | bytes 1622024 | tf_op jit(solution)/shard_map/ppermute | solution.py:132
  216.1 32.2 %collective-permute-start.17 = (f32[1,256]{1,0:T(1,128)S(1)}, f32[1,256]{1,0:T(1,128)S(1)}, u32[]{:S(2)}, u32[]{:S(2)}) collective-permute-start(f32[1,256]{1,0:T(1,128)S(1)} %get-tuple-element.140), channel_id=1, source_target_pairs={{0,4},{4,8},{8,12},{12,16},{16,20},{20,24},{24,28},{1,5},{5,9},{9,... | collective-permute-start | bytes 3080 | tf_op jit(solution)/shard_map/ppermute | solution.py:370
  246.4 3.2 collective-permute-start.18
  248.3 76.0 %collective-permute-start.46 = (f32[768,256]{1,0:T(8,128)}, f32[768,256]{1,0:T(8,128)S(1)}, u32[]{:S(2)}, u32[]{:S(2)}) collective-permute-start(f32[768,256]{1,0:T(8,128)} %get-tuple-element.129), channel_id=1, source_target_pairs={{0,8},{1,9},{2,10},{3,11},{4,12},{5,13},{6,14},{7,15},{8,0},{9,1},... | collective-permute-start | bytes 2359304 | tf_op jit(solution)/shard_map/ppermute | solution.py:132
  249.6 24.5 %collective-permute-start.15 = (f32[1,256]{1,0:T(1,128)S(1)}, f32[1,256]{1,0:T(1,128)S(1)}, u32[]{:S(2)}, u32[]{:S(2)}) collective-permute-start(f32[1,256]{1,0:T(1,128)S(1)} %get-tuple-element.142), channel_id=1, source_target_pairs={{0,4},{4,8},{8,12},{12,16},{16,20},{20,24},{24,28},{1,5},{5,9},{9,... | collective-permute-start | bytes 3080 | tf_op jit(solution)/shard_map/ppermute | solution.py:370
  274.1 3.2 collective-permute-start.16
  277.3 20.6 %collective-permute-start.40 = (f32[256,256]{1,0:T(8,128)}, f32[256,256]{1,0:T(8,128)S(1)}, u32[]{:S(2)}, u32[]{:S(2)}) collective-permute-start(f32[256,256]{1,0:T(8,128)} %get-tuple-element.122), channel_id=1, source_target_pairs={{0,1},{1,0},{2,3},{3,2},{4,5},{5,4},{6,7},{7,6},{8,9},{9,8},{10,11... | collective-permute-start | bytes 786440 | tf_op jit(solution)/shard_map/ppermute | solution.py:132
  278.0 52.3 %collective-permute-start.47 = (f32[768,256]{1,0:T(8,128)}, f32[768,256]{1,0:T(8,128)S(1)}, u32[]{:S(2)}, u32[]{:S(2)}) collective-permute-start(f32[768,256]{1,0:T(8,128)} %get-tuple-element.130), channel_id=1, source_target_pairs={{0,16},{1,17},{2,18},{3,19},{4,20},{5,21},{6,22},{7,23},{8,24},{9,... | collective-permute-start | bytes 2359304 | tf_op jit(solution)/shard_map/ppermute | solution.py:132
  278.0 79.8 %collective-permute-start.48 = (f32[768,256]{1,0:T(8,128)}, f32[768,256]{1,0:T(8,128)S(1)}, u32[]{:S(2)}, u32[]{:S(2)}) collective-permute-start(f32[768,256]{1,0:T(8,128)} %get-tuple-element.131), channel_id=1, source_target_pairs={{0,24},{1,25},{2,26},{3,27},{4,28},{5,29},{6,30},{7,31},{8,16},{9,... | collective-permute-start | bytes 2359304 | tf_op jit(solution)/shard_map/ppermute | solution.py:132
  279.7 24.5 %copy-start.34 = (f32[256,256]{1,0:T(8,128)S(1)}, f32[256,256]{1,0:T(8,128)}, u32[]{:S(2)}) copy-start(f32[256,256]{1,0:T(8,128)} %get-tuple-element.124) | copy-start | bytes 786436
  294.6 7.3 %collective-permute-start.38 = (f32[128,128]{1,0:T(8,128)}, f32[128,128]{1,0:T(8,128)S(1)}, u32[]{:S(2)}, u32[]{:S(2)}) collective-permute-start(f32[128,128]{1,0:T(8,128)} %get-tuple-element.118), channel_id=1, source_target_pairs={{0,1},{1,2},{2,3},{4,5},{5,6},{6,7},{8,9},{9,10},{10,11},{12,13},{... | collective-permute-start | bytes 196616 | tf_op jit(solution)/shard_map/ppermute | solution.py:370
  297.9 18.1 %copy-start.26 = (f32[256,256]{1,0:T(8,128)}, f32[256,256]{1,0:T(8,128)S(1)}, u32[]{:S(2)}) copy-start(f32[256,256]{1,0:T(8,128)S(1)} %collective-permute-done.40.refs_1_) | copy-start | bytes 786436
  297.9 6.4 %collective-permute-start.39 = (f32[128,128]{1,0:T(8,128)}, f32[128,128]{1,0:T(8,128)S(1)}, u32[]{:S(2)}, u32[]{:S(2)}) collective-permute-start(f32[128,128]{1,0:T(8,128)} %get-tuple-element.119), channel_id=1, source_target_pairs={{1,0},{2,1},{3,2},{5,4},{6,5},{7,6},{9,8},{10,9},{11,10},{13,12},{... | collective-permute-start | bytes 196616 | tf_op jit(solution)/shard_map/ppermute | solution.py:370
  301.9 14.8 %collective-permute-start.41 = (f32[256,256]{1,0:T(8,128)}, f32[256,256]{1,0:T(8,128)S(1)}, u32[]{:S(2)}, u32[]{:S(2)}) collective-permute-start(f32[256,256]{1,0:T(8,128)} %get-tuple-element.123), channel_id=1, source_target_pairs={{0,2},{1,3},{2,0},{3,1},{4,6},{5,7},{6,4},{7,5},{8,10},{9,11},{10,... | collective-permute-start | bytes 786440 | tf_op jit(solution)/shard_map/ppermute | solution.py:132
  304.3 12.4 %collective-permute-start.42 = (f32[256,256]{1,0:T(8,128)S(1)}, f32[256,256]{1,0:T(8,128)S(1)}, u32[]{:S(2)}, u32[]{:S(2)}) collective-permute-start(f32[256,256]{1,0:T(8,128)S(1)} %copy-done.34), channel_id=1, source_target_pairs={{0,3},{1,2},{2,1},{3,0},{4,7},{5,6},{6,5},{7,4},{8,11},{9,10},{10,... | collective-permute-start | bytes 786440 | tf_op jit(solution)/shard_map/ppermute | solution.py:132
  321.0 46.7 %collective-permute-start.43 = (f32[256,256]{1,0:T(8,128)}, f32[256,256]{1,0:T(8,128)S(1)}, u32[]{:S(2)}, u32[]{:S(2)}) collective-permute-start(f32[256,256]{1,0:T(8,128)} %get-tuple-element.126), channel_id=1, source_target_pairs={{0,8},{1,9},{2,10},{3,11},{4,12},{5,13},{6,14},{7,15},{8,0},{9,1},... | collective-permute-start | bytes 786440 | tf_op jit(solution)/shard_map/ppermute | solution.py:132
  324.3 43.4 %collective-permute-start.44 = (f32[256,256]{1,0:T(8,128)}, f32[256,256]{1,0:T(8,128)S(1)}, u32[]{:S(2)}, u32[]{:S(2)}) collective-permute-start(f32[256,256]{1,0:T(8,128)} %get-tuple-element.127), channel_id=1, source_target_pairs={{0,16},{1,17},{2,18},{3,19},{4,20},{5,21},{6,22},{7,23},{8,24},{9,... | collective-permute-start | bytes 786440 | tf_op jit(solution)/shard_map/ppermute | solution.py:132
  324.3 33.5 %copy-start.5 = (f32[768,256]{1,0:T(8,128)}, f32[768,256]{1,0:T(8,128)S(1)}, u32[]{:S(2)}) copy-start(f32[768,256]{1,0:T(8,128)S(1)} %collective-permute-done.46.refs_1_) | copy-start | bytes 2359300
  324.3 44.7 %collective-permute-start.45 = (f32[256,256]{1,0:T(8,128)}, f32[256,256]{1,0:T(8,128)S(1)}, u32[]{:S(2)}, u32[]{:S(2)}) collective-permute-start(f32[256,256]{1,0:T(8,128)} %get-tuple-element.128), channel_id=1, source_target_pairs={{0,24},{1,25},{2,26},{3,27},{4,28},{5,29},{6,30},{7,31},{8,16},{9,... | collective-permute-start | bytes 786440 | tf_op jit(solution)/shard_map/ppermute | solution.py:132
  330.3 27.5 %copy-start.6 = (f32[768,256]{1,0:T(8,128)}, f32[768,256]{1,0:T(8,128)S(1)}, u32[]{:S(2)}) copy-start(f32[768,256]{1,0:T(8,128)S(1)} %collective-permute-done.47.refs_2_) | copy-start | bytes 2359300
  (25 other events, 54.4 us)

commit v2 on v1

--- a/solution.py
+++ b/solution.py
@@ -15,8 +15,8 @@
 
 AXES = ("gx", "gy")
 ANY = pl.BlockSpec(memory_space=pl.ANY)
-SMEM = pl.BlockSpec(memory_space=pltpu.SMEM)
 f32 = jnp.float32
+WHOLE = pltpu.CompilerParams(vmem_limit_bytes=67043328)
 
 
 def sds(*shape):
@@ -32,7 +32,7 @@
     return pl.CostEstimate(flops=flops, bytes_accessed=nbytes, transcendentals=0)
 
 
-def split_slab(me, parts, after, H, C):
+def split_slab(parts, after, H, C, far=1):
     arrays, steps, N = [], [], 0
     for members, (lv0, lv1), (r0, r1) in parts:
         for a in members:
@@ -43,29 +43,34 @@
                 steps.append((t, lv, r0, r1 - r0, N))
                 N += r1 - r0
     nb = arrays[0].shape[1]
-
-    def kernel(me_ref, *refs):
+    work = [(e, one) for e in range(far) for one in steps]
+
+    def kernel(*refs):
         ins = refs[: len(arrays)]
-        outs = refs[len(arrays) + len(after) :][:H]
-        stage, sem_in, sem_out = refs[len(arrays) + len(after) + H :]
-        core, own = lax.rem(me_ref[0], nb), me_ref[1]
+        outs = refs[len(arrays) + len(after) :][: far * H]
+        stage, sem_in, sem_out = refs[len(arrays) + len(after) + far * H :]
+        core, own = lax.rem(lax.axis_index("gx"), nb), lax.axis_index("gy")
         loads = []
-        for n, (t, lv, r0, rows, off) in enumerate(steps):
+        for n, (e, (t, lv, r0, rows, off)) in enumerate(work):
             loads.append(
                 pltpu.make_async_copy(
-                    ins[t].at[lv, core, pl.ds(r0, rows), :], stage.at[pl.ds(off, rows), :], sem_in.at[n]
+                    ins[t].at[lv, lax.bitwise_xor(core, e), pl.ds(r0, rows), :],
+                    stage.at[e, pl.ds(off, rows), :],
+                    sem_in.at[n],
                 )
             )
             loads[-1].start()
         stores = []
-        for n, (t, lv, r0, rows, off) in enumerate(steps):
+        for n, (e, (t, lv, r0, rows, off)) in enumerate(work):
             loads[n].wait()
             for m in [*range(1, H), 0]:
                 block = lax.bitwise_xor(own, m)
                 cols = pl.ds(pl.multiple_of(block * C, C), C)
                 stores.append(
                     pltpu.make_async_copy(
-                        stage.at[pl.ds(off, rows), cols], outs[m].at[pl.ds(off, rows), :], sem_out.at[n, m]
+                        stage.at[e, pl.ds(off, rows), cols],
+                        outs[e * H + m].at[pl.ds(off, rows), :],
+                        sem_out.at[n, m],
                     )
                 )
                 stores[-1].start()
@@ -74,27 +79,37 @@
 
     return pl.pallas_call(
         kernel,
-        out_shape=[sds(N, C)] * H,
-        in_specs=[SMEM] + [ANY] * (len(arrays) + len(after)),
-        out_specs=[ANY] * H,
+        out_shape=[sds(N, C)] * (far * H),
+        in_specs=[ANY] * (len(arrays) + len(after)),
+        out_specs=[ANY] * (far * H),
         scratch_shapes=[
-            pltpu.VMEM((N, H * C), f32),
-            pltpu.SemaphoreType.DMA((len(steps),)),
-            pltpu.SemaphoreType.DMA((len(steps), H)),
+            pltpu.VMEM((far, N, H * C), f32),
+            pltpu.SemaphoreType.DMA((len(work),)),
+            pltpu.SemaphoreType.DMA((len(work), H)),
         ],
-        cost_estimate=cost(8 * N * H * C),
-    )(me, *arrays, *after)
-
-
-def regroup(me, pieces, after, H, nb):
-    N, C = pieces[0].shape
-
-    def kernel(me_ref, *refs):
-        ins, outs = refs[:H], refs[H + len(after) :][:H]
-        stage, sem_in, sem_out = refs[H + len(after) + H :]
-        z, j = lax.div(me_ref[0], nb), me_ref[1]
+        compiler_params=WHOLE,
+        cost_estimate=cost(8 * far * N * H * C),
+    )(*arrays, *after)
+
+
+def regroup(pieces, after, H, nb):
+    C = pieces[0][0].shape[1]
+    rows = [group[0].shape[0] for group in pieces]
+    N = sum(rows)
+    flat = [p for group in pieces for p in group]
+
+    def kernel(*refs):
+        ins, outs = refs[: len(flat)], refs[len(flat) + len(after) :][:H]
+        stage, sem_in, sem_out = refs[len(flat) + len(after) + H :]
+        z, j = lax.div(lax.axis_index("gx"), nb), lax.axis_index("gy")
         loads = [
-            pltpu.make_async_copy(ins[m], stage.at[lax.bitwise_xor(j, m)], sem_in.at[m]) for m in range(H)
+            pltpu.make_async_copy(
+                ins[g * H + m],
+                stage.at[lax.bitwise_xor(j, m), pl.ds(sum(rows[:g]), rows[g]), :],
+                sem_in.at[g * H + m],
+            )
+            for g in range(len(rows))
+            for m in range(H)
         ]
         for c in loads:
             c.start()
@@ -102,7 +117,7 @@
             c.wait()
         stores = [
             pltpu.make_async_copy(stage.at[lax.bitwise_xor(z, q)], outs[q], sem_out.at[q])
-            for q in far_first(H) + [0]
+            for q in partners(H) + [0]
         ]
         for c in stores:
             c.start()
@@ -112,19 +127,20 @@
     return pl.pallas_call(
         kernel,
         out_shape=[sds(N, C)] * H,
-        in_specs=[SMEM] + [ANY] * (H + len(after)),
+        in_specs=[ANY] * (len(flat) + len(after)),
         out_specs=[ANY] * H,
         scratch_shapes=[
             pltpu.VMEM((H, N, C), f32),
-            pltpu.SemaphoreType.DMA((H,)),
+            pltpu.SemaphoreType.DMA((len(flat),)),
             pltpu.SemaphoreType.DMA((H,)),
         ],
+        compiler_params=WHOLE,
         cost_estimate=cost(8 * H * N * C),
-    )(me, *pieces, *after)
-
-
-def far_first(H):
-    return sorted(range(1, H), key=lambda q: (-q.bit_length(), q))
+    )(*flat, *after)
+
+
+def partners(H):
+    return list(range(1, H))
 
 
 def moved(x, G, H, ds, dr):
@@ -132,15 +148,15 @@
     return lax.ppermute(x, AXES, pairs)
 
 
-def coefficients(me, chunks, layout, planes, rims, after, G, H, L, R, C):
+def coefficients(chunks, layout, planes, rims, after, G, H, L, R, C):
     nz = G * L
     wide = -(-nz // 128) * 128
     flat = [p for chunk in chunks for p in chunk]
 
-    def kernel(me_ref, terrain, mass, land, top, rim_t, rim_m, *refs):
+    def kernel(terrain, mass, land, top, rim_t, rim_m, *refs):
         ins = refs[: len(flat)]
         geo, couple, inv, rim, west, east, th, pr, ra, sem = refs[len(flat) + len(after) :]
-        i = me_ref[0]
+        i = lax.axis_index("gx")
         copies = []
         for c, parts in enumerate(layout):
             for q in range(H):
@@ -208,7 +224,7 @@
     return pl.pallas_call(
         kernel,
         out_shape=[sds(nz, R, C)] * 3 + [sds(nz, 2, C)] + [sds(R, wide)] * 2,
-        in_specs=[SMEM] + [VM] * 6 + [ANY] * (len(flat) + len(after)),
+        in_specs=[VM] * 6 + [ANY] * (len(flat) + len(after)),
         out_specs=[VM] * 6,
         scratch_shapes=[
             pltpu.VMEM((nz, R, C), f32),
@@ -217,14 +233,14 @@
             pltpu.SemaphoreType.DMA((ncopy,)),
         ],
         cost_estimate=cost(24 * nz * R * C, 60 * nz * R * C),
-    )(me, *planes, *rims, *flat, *after)
-
-
-def lifted(me, geo, rim, west, east, after):
+    )(*planes, *rims, *flat, *after)
+
+
+def lifted(geo, rim, west, east, after):
     nz, R, C = geo.shape
     deep = 4 if nz % 4 == 0 else 1
 
-    def kernel(me_ref, geo_ref, rim_ref, west_ref, east_ref, *refs):
+    def kernel(geo_ref, rim_ref, west_ref, east_ref, *refs):
         out_ref = refs[-1]
         lane = lax.broadcasted_iota(jnp.int32, (R, C), 1)
         row = lax.broadcasted_iota(jnp.int32, (R, C), 0)
@@ -246,17 +262,17 @@
             kernel,
             out_shape=sds(nz, R, C),
             grid=(nz // deep,),
-            in_specs=[SMEM, block(R, C), block(2, C), side, side] + [ANY] * len(after),
+            in_specs=[block(R, C), block(2, C), side, side] + [ANY] * len(after),
             out_specs=block(R, C),
             cost_estimate=cost(8 * nz * R * C, 8 * nz * R * C),
-        )(me, geo, rim, west, east, *after)
+        )(geo, rim, west, east, *after)
     ]
 
 
-def smoothed(me, wind, before, behind, after):
+def smoothed(wind, before, behind, after):
     L, RS, Y = wind.shape
 
-    def kernel(me_ref, wind_ref, before_ref, behind_ref, *refs):
+    def kernel(wind_ref, before_ref, behind_ref, *refs):
         out_ref = refs[-1]
         lane = lax.broadcasted_iota(jnp.int32, (RS, Y), 1)
         row = lax.broadcasted_iota(jnp.int32, (RS, Y), 0)
@@ -273,48 +289,61 @@
             kernel,
             out_shape=sds(L, RS, Y),
             grid=(L,),
-            in_specs=[SMEM, block(RS), block(1), block(1)] + [ANY] * len(after),
+            in_specs=[block(RS), block(1), block(1)] + [ANY] * len(after),
             out_specs=block(RS),
             cost_estimate=cost(8 * L * RS * Y, 8 * L * RS * Y),
-        )(me, wind, before, behind, *after)
+        )(wind, before, behind, *after)
     ]
 
 
-def substitute(me, pieces, lift, couple, inv, wind, r0, rows, G, H, L, R, C):
+def substitute(pieces, lift, couple, inv, wind, r0, rows, G, H, L, R, C):
     nz = G * L
     nb = G // H
+    tall = 8
     held = [] if wind is None else [wind]
-
-    def kernel(me_ref, lift_ref, couple_ref, inv_ref, *refs):
+    pieces = [p.reshape(nb * L, rows, C) for p in pieces]
+
+    def kernel(lift_ref, couple_ref, inv_ref, *refs):
         ins = refs[:H]
-        out, fo, li, co, iv, sem = refs[H + len(held) :]
-        i = me_ref[0]
-        where = pl.ds(r0, rows)
-        copies = [
-            pltpu.make_async_copy(lift_ref.at[:, where, :], li, sem.at[G]),
-            pltpu.make_async_copy(couple_ref.at[:, where, :], co, sem.at[G + 1]),
-            pltpu.make_async_copy(inv_ref.at[:, where, :], iv, sem.at[G + 2]),
-        ]
-        for k in range(G):
-            s = lax.bitwise_xor(i, k)
-            copies.append(
-                pltpu.make_async_copy(
-                    ins[k // nb].at[pl.ds(k % nb * (L * rows), L * rows), :],
-                    fo.at[pl.ds(pl.multiple_of(s * (L * rows), 8), L * rows), :],
-                    sem.at[k],
+        out, fo, li, co, iv, sem, sem_out = refs[H + len(held) :]
+        i = lax.axis_index("gx")
+
+        def loads(b):
+            part = pl.ds(pl.multiple_of(b * tall, tall), tall)
+            where = pl.ds(pl.multiple_of(r0 + b * tall, tall), tall)
+            copies = []
+            for src, dst in ((lift_ref, li), (couple_ref, co), (inv_ref, iv)):
+                copies.append(
+                    pltpu.make_async_copy(src.at[:, where, :], dst.at[:, part, :], sem.at[b, len(copies)])
                 )
-            )
-        for c in copies:
-            c.start()
-        for c in copies:
-            c.wait()
-
-        def step(b, _):
-            base = pl.multiple_of(b * 8, 8)
-            part = pl.ds(base, 8)
-            value = jnp.zeros((8, C), f32)
+            for k in range(G):
+                s = lax.bitwise_xor(i, k)
+                copies.append(
+                    pltpu.make_async_copy(
+                        ins[k // nb].at[pl.ds(k % nb * L, L), part, :],
+                        fo.at[pl.ds(s * L, L), part, :],
+                        sem.at[b, len(copies)],
+                    )
+                )
+            return copies
+
+        def store(b):
+            part = pl.ds(pl.multiple_of(b * tall, tall), tall)
+            where = pl.ds(pl.multiple_of(r0 + b * tall, tall), tall)
+            return pltpu.make_async_copy(li.at[:, part, :], out.at[:, where, :], sem_out.at[b])
+
+        def begin(b, _):
+            for c in loads(b):
+                c.start()
+            return 0
+
+        def sweep(b, _):
+            for c in loads(b):
+                c.wait()
+            part = pl.ds(pl.multiple_of(b * tall, tall), tall)
+            value = jnp.zeros((tall, C), f32)
             for k in range(nz):
-                force = fo[pl.ds(pl.multiple_of(k * rows + base, 8), 8), :] + li[k, part, :]
+                force = fo[k, part, :] + li[k, part, :]
                 if k:
                     force = force + co[k - 1, part, :] * value
                 value = force * iv[k, part, :]
@@ -322,28 +351,30 @@
             for k in range(nz - 2, -1, -1):
                 value = li[k, part, :] + (co[k, part, :] * iv[k, part, :]) * value
                 li[k, part, :] = value
+            store(b).start()
             return 0
 
-        lax.fori_loop(0, rows // 8, step, 0)
-        done = pltpu.make_async_copy(li, out.at[:, where, :], sem.at[G + 3])
-        done.start()
-        done.wait()
+        def finish(b, _):
+            store(b).wait()
+            return 0
+
+        for stage in (begin, sweep, finish):
+            lax.fori_loop(0, rows // tall, stage, 0)
 
     return pl.pallas_call(
         kernel,
         out_shape=sds(nz, R, C),
-        in_specs=[SMEM] + [ANY] * (3 + H + len(held)),
+        in_specs=[ANY] * (3 + H + len(held)),
         out_specs=ANY,
-        scratch_shapes=[
-            pltpu.VMEM((nz * rows, C), f32),
-            pltpu.VMEM((nz, rows, C), f32),
-            pltpu.VMEM((nz, rows, C), f32),
-            pltpu.VMEM((nz, rows, C), f32),
-            pltpu.SemaphoreType.DMA((G + 4,)),
+        scratch_shapes=[pltpu.VMEM((nz, rows, C), f32)] * 4
+        + [
+            pltpu.SemaphoreType.DMA((rows // tall, G + 3)),
+            pltpu.SemaphoreType.DMA((rows // tall,)),
         ],
-        input_output_aliases={4 + H: 0} if held else {},
+        input_output_aliases={3 + H: 0} if held else {},
+        compiler_params=WHOLE,
         cost_estimate=cost(20 * nz * rows * C, 8 * nz * rows * C),
-    )(me, lift, couple, inv, *pieces, *held)
+    )(lift, couple, inv, *pieces, *held)
 
 
 def on_device(theta, pressure, vertical_wind, terrain, column_mass, land_mask, pbl_top):
@@ -351,13 +382,11 @@
     nb = G // H
     L, RS, Y = theta.shape
     R, C = RS // nb, Y // H
-    s, r = lax.axis_index("gx"), lax.axis_index("gy")
-    me = jnp.stack([s, r]).astype(jnp.int32)
     slab = lambda a: a.reshape(a.shape[0], nb, -1, Y)
     after = []
 
     def step(kernel, *args):
-        out = kernel(me, *args)
+        out = kernel(*args)
         after[:] = [out[0]]
         return out
 
@@ -372,14 +401,17 @@
     def family(a):
         return [slab(a)] + [slab(send_to(a, e, 0)) for e in range(1, nb)]
 
-    def cut(parts):
-        pieces = step(split_slab, parts, list(after), H, C)
-        return [pieces[0]] + [send_to(pieces[m], 0, m) for m in range(1, H)]
+    def cut(parts, far=1):
+        pieces = step(split_slab, parts, list(after), H, C, far)
+        out = [pieces[0]] + [send_to(pieces[m], 0, m) for m in range(1, H)]
+        for e in range(1, far):
+            out += [send_to(pieces[e * H + m], e, m) for m in range(H)]
+        return [out[e * H : e * H + H] for e in range(far)]
 
     def send(pieces, behind_of=()):
         pieces = step(regroup, pieces, [*after, *behind_of], H, nb)
         out = [pieces[0]] + [None] * (H - 1)
-        for q in far_first(H):
+        for q in partners(H):
             out[q] = send_to(pieces[q], q * nb, 0)
         return out
 
@@ -387,13 +419,11 @@
         return lax.optimization_barrier((*x, *after))[: len(x)]
 
     full = (0, R)
-    first = cut([(family(theta[:1]), (0, 1), full)])
-
-    th = family(later(theta)[0])
+    th = family(theta)
+    first = cut([([slab(theta)], (0, 1), full)], nb)
     mid_levels = max(1, min(3, L - 1))
     second = cut([(th, (1, mid_levels), full)]) if mid_levels > 1 else None
-    sources = later(pressure)
-    pr = family(sources[0])
+    pr = family(later(pressure)[0])
     lead = [send(first)]
     layout = [[(0, e, 0, 1, e * R) for e in range(nb)]]
 
@@ -408,6 +438,12 @@
         lead.append(send(second))
         n = mid_levels - 1
         layout.append([(0, e, 1, n, e * n * R) for e in range(nb)])
+    lead.append(send(third))
+    n, base = L - mid_levels, nb * (L - mid_levels) * R
+    layout.append(
+        [(0, e, mid_levels, n, e * n * R) for e in range(nb)]
+        + [(1, e, 0, half, base + e * half * R) for e in range(nb)]
+    )
 
     blown = step(smoothed, vertical_wind, before[2], behind[2], list(after))[0]
     safe = lambda p: jnp.where(p > 0, p, 1.0)
@@ -427,37 +463,33 @@
     rim, blown = family(rim), family(blown)
 
     fourth = cut([(pr, (half, L), full), (rim, (0, 1), (0, tall))])
-    lead.append(send(third))
+    part, last = max(8, R // 4 // 8 * 8), max(8, R // 4 // 8 * 8)
+    marks = sorted({0, min(part, R), max(R - last, min(part, R)), R})
+    rows_cut = list(zip(marks[:-1], marks[1:]))
+    cuts = [cut([(blown, (0, L), rows_cut[0])])]
+    lead.append(send(fourth))
     plane_rim = lambda a: jnp.concatenate([beside(a[-1:], "gx", True), beside(a[:1], "gx", False)], 0)
     rim_planes = [plane_rim(a) for a in later(terrain, column_mass)]
-    n, base = L - mid_levels, nb * (L - mid_levels) * R
-    layout.append(
-        [(0, e, mid_levels, n, e * n * R) for e in range(nb)]
-        + [(1, e, 0, half, base + e * half * R) for e in range(nb)]
-    )
-    last = max(8, R // 4 // 8 * 8)
-    rows_cut = [(0, R - last), (R - last, R)]
-    cuts = [cut([(blown, (0, L), rows_cut[0])])]
-    lead.append(send(fourth))
     n = L - half
     layout.append(
         [(1, e, half, n, e * n * R) for e in range(nb)]
         + [(2, e, 0, 1, nb * n * R + e * tall) for e in range(nb)]
     )
-    cuts.append(cut([(blown, (0, L), rows_cut[1])]))
+    cuts += [cut([(blown, (0, L), rows)]) for rows in rows_cut[1:]]
     winds = [send(cuts[0], lead[-2][1:])]
+    winds += [send(pieces, lead[-1][1:]) for pieces in cuts[1:-1]]
 
     planes = (terrain, column_mass, land_mask, pbl_top)
     geo, couple, inv, rim_geo, west, east = step(
         coefficients, lead, layout, planes, rim_planes, list(after), G, H, L, R, C
     )
     west, east = beside(east, "gy", True), beside(west, "gy", False)
+    winds += [send(pieces) for pieces in cuts[len(winds) :]]
     lift = step(lifted, geo, rim_geo, west, east, list(after))[0]
-    winds.append(send(cuts[1]))
 
     wind = None
     for (r0, r1), pieces in zip(rows_cut, winds):
-        wind = substitute(me, pieces, lift, couple, inv, wind, r0, r1 - r0, G, H, L, R, C)
+        wind = substitute(pieces, lift, couple, inv, wind, r0, r1 - r0, G, H, L, R, C)
     return wind, geo
 
 

time: 378 us -> 434 us (1.15)
  waiting for transfers between devices: 184 us -> 255 us
  local copies, waits for them, and re-layouts: 15.5 us -> 8.09 us
  Pallas kernels: 85.4 us -> 79.9 us
    ppermute x41 -> x50, waiting for transfers between devices: 174 us -> 232 us  [moved(): return lax.ppermute(x, AXES, pairs)]
    ppermute x8, starting transfers between devices: 38.3 us -> 21.8 us  [beside(): return lax.ppermute(x, axis, pairs)]
    ppermute x8, waiting for transfers between devices: 10.1 us -> 23.4 us  [beside(): return lax.ppermute(x, axis, pairs)]
    ppermute x41 -> x50, starting transfers between devices: 46.5 us -> 59.6 us  [moved(): return lax.ppermute(x, AXES, pairs)]
    unnamed x81 -> x5, local copies, waits for them, and re-layouts: 9.36 us -> 1.25 us
    pallas_call x15 -> x18, Pallas kernels: 61.3 us -> 55.8 us  [the longest x7 19.5 us: regroup(): pl.pallas_call(kernel, out_shape=[sds(N, C)] * H, in_specs=[ANY] * (len(f...]
  transfers between devices with their start and end apart: 49 -> 58, of which waited for: 23 -> 24; matrix products, arithmetic and copies ran while one was open for 2% -> 3% of each run, Pallas kernels for 18% -> 15%
where the time goes in v2:
time: 434 us; the launch traced here: 432 us
  waiting for transfers between devices  255 us (59%)
  starting transfers between devices  81.4 us (19%)
  Pallas kernels  79.9 us (18%)
  local copies, waits for them, and re-layouts  8.09 us (2%)
  other arithmetic  6.6 us (2%)
    ppermute x50, waiting for transfers between devices, moved(): return lax.ppermute(x, AXES, pairs)  232 us
    ppermute x50, starting transfers between devices, moved(): return lax.ppermute(x, AXES, pairs)  59.6 us
    ppermute x8, waiting for transfers between devices, beside(): return lax.ppermute(x, axis, pairs)  23.4 us
    ppermute x8, starting transfers between devices, beside(): return lax.ppermute(x, axis, pairs)  21.8 us
    pallas_call x7, Pallas kernels, regroup(): pl.pallas_call(kernel, out_shape=[sds(N, C)] * H, in_specs=[ANY] * (len(f...  19.5 us
    pallas_call x7, Pallas kernels, split_slab(): pl.pallas_call(kernel, out_shape=[sds(N, C)] * (far * H), in_specs=[ANY]...  17.5 us
    pallas_call x1, Pallas kernels, coefficients(): pl.pallas_call(kernel, out_shape=[sds(nz, R, C)] * 3 + [sds(nz, 2, C)] +...  14.9 us
    pallas_call x3, Pallas kernels, substitute(): pl.pallas_call(kernel, out_shape=sds(nz, R, C), in_specs=[ANY] * (3 + H +...  12.5 us
  transfers between devices with their start and end apart: 58, of which 24 were waited for; matrix products, arithmetic and copies ran while one was open for 3% of the time, Pallas kernels for 15%

profile of v2, /device:TPU:12, one launch (start us, length us, event | category | flops | bytes accessed | tf_op | source)
XLA Modules:
  0.0 432.4 jit_solution(3305733043164260007)
XLA Ops:
  0.7 2.1 shard_map.86
  2.8 5.4 %collective-permute-done = f32[4,256,1024]{2,1,0:T(8,128)} collective-permute-done((f32[4,256,1024]{2,1,0:T(8,128)}, f32[4,256,1024]{2,1,0:T(8,128)}, u32[]{:S(2)}, u32[]{:S(2)}) %collective-permute-start) | collective-permute-done | bytes 4194336 | tf_op jit(solution)/shard_map/ppermute | solution.py:148
  8.2 2.5 shard_map.87
  13.5 2.4 collective-permute-start.4
  15.9 1.7 collective-permute-done.2.refs_1_
  19.2 12.4 %collective-permute-done.4.refs_3_ = f32[128,256]{1,0:T(8,128)} collective-permute-done((f32[128,256]{1,0:T(8,128)}, f32[128,256]{1,0:T(8,128)}, u32[]{:S(2)}, u32[]{:S(2)}) %collective-permute-start.4) | collective-permute-done | bytes 131104 | tf_op jit(solution)/shard_map/ppermute | solution.py:148
  31.7 2.6 collective-permute-start.8
  35.8 4.6 %collective-permute-done.7.refs_6_ = f32[128,256]{1,0:T(8,128)} collective-permute-done((f32[128,256]{1,0:T(8,128)}, f32[128,256]{1,0:T(8,128)}, u32[]{:S(2)}, u32[]{:S(2)}) %collective-permute-start.7) | collective-permute-done | bytes 131104 | tf_op jit(solution)/shard_map/ppermute | solution.py:148
  40.4 2.5 collective-permute-start.16
  43.0 2.4 shard_map.88
  45.4 3.0 shard_map.89
  50.5 2.6 collective-permute-start.13
  54.8 8.3 %collective-permute-done.15.refs_2_ = f32[512,256]{1,0:T(8,128)} collective-permute-done((f32[512,256]{1,0:T(8,128)}, f32[512,256]{1,0:T(8,128)}, u32[]{:S(2)}, u32[]{:S(2)}) %collective-permute-start.15) | collective-permute-done | bytes 524320 | tf_op jit(solution)/shard_map/ppermute | solution.py:148
  63.1 3.4 collective-permute-start.9
  67.1 3.3 collective-permute-start.10
  70.5 3.0 shard_map.90
  73.4 17.5 %collective-permute-done.9 = f32[3,4,1,1024]{3,2,1,0:T(1,128)} collective-permute-done((f32[3,4,1,1024]{3,2,1,0:T(1,128)}, f32[3,4,1,1024]{3,2,1,0:T(1,128)}, u32[]{:S(2)}, u32[]{:S(2)}) %collective-permute-start.9) | collective-permute-done | bytes 49184 | tf_op jit(solution)/shard_map/ppermute | solution.py:399
  93.6 4.1 collective-permute-done.12.refs_2_
  97.8 3.6 shard_map.91
  101.4 6.3 %shard_map.92.refs_4_ = f32[4,256,1024]{2,1,0:T(8,128)} custom-call(f32[4,256,1024]{2,1,0:T(8,128)} %wind_ref.1, f32[4,1,1024]{2,1,0:T(1,128)} %slice_bitcast_fusion.1.before_ref, f32[4,1,1024]{2,1,0:T(1,128)} %slice_bitcast_fusion.behind_ref, f32[768,256]{1,0:T(8,128)} %get-tuple-element.100.refs_0_.refs_8_), custom_call_target="tpu_custom_call" | custom-call | flops 8388608 | bytes 8388608 | tf_op jit(solution)/shard_map/pallas_call | solution.py:288
  111.8 2.8 collective-permute-start.27
  115.8 2.7 shard_map.93
  120.2 12.7 %collective-permute-done.27.refs_2_ = f32[256,256]{1,0:T(8,128)} collective-permute-done((f32[256,256]{1,0:T(8,128)}, f32[256,256]{1,0:T(8,128)}, u32[]{:S(2)}, u32[]{:S(2)}) %collective-permute-start.27) | collective-permute-done | bytes 262176 | tf_op jit(solution)/shard_map/ppermute | solution.py:148
  132.9 5.8 %collective-permute-done.28.refs_3_ = f32[256,256]{1,0:T(8,128)} collective-permute-done((f32[256,256]{1,0:T(8,128)}, f32[256,256]{1,0:T(8,128)}, u32[]{:S(2)}, u32[]{:S(2)}) %collective-permute-start.28) | collective-permute-done | bytes 262176 | tf_op jit(solution)/shard_map/ppermute | solution.py:148
  140.9 2.5 collective-permute-start.32
  143.4 2.7 collective-permute-start.33
  146.1 11.7 %collective-permute-done.19.refs_2_ = f32[528,256]{1,0:T(8,128)} collective-permute-done((f32[528,256]{1,0:T(8,128)}, f32[528,256]{1,0:T(8,128)}, u32[]{:S(2)}, u32[]{:S(2)}) %collective-permute-start.19) | collective-permute-done | bytes 540704 | tf_op jit(solution)/shard_map/ppermute | solution.py:148
  158.2 4.3 collective-permute-start.30
  162.4 1.6 collective-permute-start.31
  164.1 2.3 shard_map.94
  166.4 3.0 shard_map.95
  169.4 2.6 shard_map.96
  172.0 76.6 %collective-permute-done.30.refs_6_ = f32[512,256]{1,0:T(8,128)} collective-permute-done((f32[512,256]{1,0:T(8,128)}, f32[512,256]{1,0:T(8,128)}, u32[]{:S(2)}, u32[]{:S(2)}) %collective-permute-start.30) | collective-permute-done | bytes 524320 | tf_op jit(solution)/shard_map/ppermute | solution.py:148
  249.6 9.6 %collective-permute-done.31.refs_7_ = f32[512,256]{1,0:T(8,128)} collective-permute-done((f32[512,256]{1,0:T(8,128)}, f32[512,256]{1,0:T(8,128)}, u32[]{:S(2)}, u32[]{:S(2)}) %collective-permute-start.31) | collective-permute-done | bytes 524320 | tf_op jit(solution)/shard_map/ppermute | solution.py:148
  259.3 1.6 collective-permute-start.41
  261.2 1.5 collective-permute-start.43
  263.5 1.9 collective-permute-start.24
  265.4 3.1 collective-permute-done.24
  268.5 1.9 collective-permute-start.25
  271.7 3.8 collective-permute-start.22
  278.0 1.8 collective-permute-start.40
  279.8 2.9 collective-permute-start.36
  283.3 2.3 shard_map.97
  285.6 16.6 %collective-permute-done.39.refs_2_ = f32[512,256]{1,0:T(8,128)} collective-permute-done((f32[512,256]{1,0:T(8,128)}, f32[512,256]{1,0:T(8,128)}, u32[]{:S(2)}, u32[]{:S(2)}) %collective-permute-start.39) | collective-permute-done | bytes 524320 | tf_op jit(solution)/shard_map/ppermute | solution.py:148
  304.1 2.3 shard_map.98
  306.4 1.6 collective-permute-start.48
  308.1 10.9 %collective-permute-done.36.refs_6_.refs_14_ = f32[528,256]{1,0:T(8,128)} collective-permute-done((f32[528,256]{1,0:T(8,128)}, f32[528,256]{1,0:T(8,128)}, u32[]{:S(2)}, u32[]{:S(2)}) %collective-permute-start.36) | collective-permute-done | bytes 540704 | tf_op jit(solution)/shard_map/ppermute | solution.py:148
  318.9 2.5 collective-permute-start.55
  321.4 8.0 %collective-permute-done.37.refs_7_.refs_15_ = f32[528,256]{1,0:T(8,128)} collective-permute-done((f32[528,256]{1,0:T(8,128)}, f32[528,256]{1,0:T(8,128)}, u32[]{:S(2)}, u32[]{:S(2)}) %collective-permute-start.37) | collective-permute-done | bytes 540704 | tf_op jit(solution)/shard_map/ppermute | solution.py:148
  329.4 1.9 collective-permute-start.23
  331.3 3.0 shard_map.99
  334.4 1.9 collective-permute-start.56
  342.8 14.9 %shard_map.100 = (f32[32,128,256]{2,1,0:T(8,128)}, f32[32,128,256]{2,1,0:T(8,128)}, f32[32,128,256]{2,1,0:T(8,128)}, f32[32,2,256]{2,1,0:T(2,128)}, f32[128,128]{1,0:T(8,128)}, /*index=5*/f32[128,128]{1,0:T(8,128)}) custom-call(f32[128,256]{1,0:T(8,128)} %terrain.1, f32[128,256]{1,0:T(8,128)} %mass.1, s32[128,256]{1,0:T(8,128)} %land.1, s32[128,256]{1,0:T(8,128)} %top.1, ...), custom_call_target="tpu_custom_call" | custom-call | flops 62914560 | bytes 25165824 | tf_op jit(solution)/shard_map/pallas_call | solution.py:224
  357.7 2.8 collective-permute-start.44
  360.5 24.3 %collective-permute-done.57 = f32[256,256]{1,0:T(8,128)} collective-permute-done((f32[256,256]{1,0:T(8,128)}, f32[256,256]{1,0:T(8,128)}, u32[]{:S(2)}, u32[]{:S(2)}) %collective-permute-start.57) | collective-permute-done | bytes 262176 | tf_op jit(solution)/shard_map/ppermute | solution.py:148
  384.7 2.8 collective-permute-start.45
  387.6 2.3 shard_map.101
  391.7 1.7 collective-permute-start.51
  393.4 9.2 %shard_map.102.lift_ref = f32[32,128,256]{2,1,0:T(8,128)} custom-call(f32[32,128,256]{2,1,0:T(8,128)} %get-tuple-element.77.refs_4_.geo_ref, f32[32,2,256]{2,1,0:T(2,128)} %get-tuple-element.136.rim_ref, f32[128,128]{1,0:T(8,128)} %collective-permute-done.44.west_ref, f32[128,128]{1,0:T(8,128)} %collective-permute-done.45.east_ref, ...), custom_call_target="tpu_custom_call" | custom-call | flops 8388608 | bytes 8388608 | tf_op jit(solution)/shard_map/pallas_call | solution.py:261
  402.6 3.4 shard_map.103.refs_4_
  406.1 12.4 %collective-permute-done.54 = f32[512,256]{1,0:T(8,128)} collective-permute-done((f32[512,256]{1,0:T(8,128)}, f32[512,256]{1,0:T(8,128)}, u32[]{:S(2)}, u32[]{:S(2)}) %collective-permute-start.54) | collective-permute-done | bytes 524320 | tf_op jit(solution)/shard_map/ppermute | solution.py:148
  418.5 5.6 %shard_map.104.refs_4_ = f32[32,128,256]{2,1,0:T(8,128)} custom-call(f32[32,128,256]{2,1,0:T(8,128)} %shard_map.102.lift_ref, f32[32,128,256]{2,1,0:T(8,128)} %get-tuple-element.143.couple_ref, f32[32,128,256]{2,1,0:T(8,128)} %get-tuple-element.144.inv_ref, f32[8,64,256]{2,1,0:T(8,128)} %bitcast.53, ...), custom_call_target="tpu_custom_call", output_to_operand_aliasing={{}: (7, {})} | custom-call | flops 4194304 | bytes 10485760 | tf_op jit(solution)/shard_map/pallas_call | solution.py:364
  424.1 4.8 %collective-permute-done.51 = f32[256,256]{1,0:T(8,128)} collective-permute-done((f32[256,256]{1,0:T(8,128)}, f32[256,256]{1,0:T(8,128)}, u32[]{:S(2)}, u32[]{:S(2)}) %collective-permute-start.51) | collective-permute-done | bytes 262176 | tf_op jit(solution)/shard_map/ppermute | solution.py:148
  429.0 3.4 shard_map.105
  (95 shorter events, 39.5 us)
Async XLA Ops:
  0.6 7.6 %collective-permute-start = (f32[4,256,1024]{2,1,0:T(8,128)}, f32[4,256,1024]{2,1,0:T(8,128)}, u32[]{:S(2)}, u32[]{:S(2)}) collective-permute-start(f32[4,256,1024]{2,1,0:T(8,128)} %param.7), channel_id=1, source_target_pairs={{0,4},{1,5},{2,6},{3,7},{4,0},{5,1},{6,2},{7,3},{8,12},{9,13},{10,... | collective-permute-start | bytes 12582920 | tf_op jit(solution)/shard_map/ppermute | solution.py:148
  10.7 34.7 %collective-permute-start.1 = (f32[4,256,1024]{2,1,0:T(8,128)}, f32[4,256,1024]{2,1,0:T(8,128)}, u32[]{:S(2)}, u32[]{:S(2)}) collective-permute-start(f32[4,256,1024]{2,1,0:T(8,128)} %param.8), channel_id=1, source_target_pairs={{0,4},{1,5},{2,6},{3,7},{4,0},{5,1},{6,2},{7,3},{8,12},{9,13},{10,... | collective-permute-start | bytes 12582920 | tf_op jit(solution)/shard_map/ppermute | solution.py:148
  10.9 6.7 %collective-permute-start.2 = (f32[128,256]{1,0:T(8,128)}, f32[128,256]{1,0:T(8,128)}, u32[]{:S(2)}, u32[]{:S(2)}) collective-permute-start(f32[128,256]{1,0:T(8,128)} %get-tuple-element.81), channel_id=1, source_target_pairs={{0,1},{1,0},{2,3},{3,2},{4,5},{5,4},{6,7},{7,6},{8,9},{9,8},{10,11... | collective-permute-start | bytes 393224 | tf_op jit(solution)/shard_map/ppermute | solution.py:148
  12.4 38.1 %collective-permute-start.14 = (f32[512,256]{1,0:T(8,128)}, f32[512,256]{1,0:T(8,128)}, u32[]{:S(2)}, u32[]{:S(2)}) collective-permute-start(f32[512,256]{1,0:T(8,128)} %get-tuple-element.96), channel_id=1, source_target_pairs={{0,1},{1,0},{2,3},{3,2},{4,5},{5,4},{6,7},{7,6},{8,9},{9,8},{10,11... | collective-permute-start | bytes 1572872 | tf_op jit(solution)/shard_map/ppermute | solution.py:148
  13.0 5.5 %collective-permute-start.3 = (f32[128,256]{1,0:T(8,128)}, f32[128,256]{1,0:T(8,128)}, u32[]{:S(2)}, u32[]{:S(2)}) collective-permute-start(f32[128,256]{1,0:T(8,128)} %get-tuple-element.82), channel_id=1, source_target_pairs={{0,2},{1,3},{2,0},{3,1},{4,6},{5,7},{6,4},{7,5},{8,10},{9,11},{10,... | collective-permute-start | bytes 393224 | tf_op jit(solution)/shard_map/ppermute | solution.py:148
  13.5 18.1 %collective-permute-start.4 = (f32[128,256]{1,0:T(8,128)}, f32[128,256]{1,0:T(8,128)}, u32[]{:S(2)}, u32[]{:S(2)}) collective-permute-start(f32[128,256]{1,0:T(8,128)} %get-tuple-element.83), channel_id=1, source_target_pairs={{0,3},{1,2},{2,1},{3,0},{4,7},{5,6},{6,5},{7,4},{8,11},{9,10},{10,... | collective-permute-start | bytes 393224 | tf_op jit(solution)/shard_map/ppermute | solution.py:148
  17.6 14.0 %collective-permute-start.5 = (f32[128,256]{1,0:T(8,128)}, f32[128,256]{1,0:T(8,128)}, u32[]{:S(2)}, u32[]{:S(2)}) collective-permute-start(f32[128,256]{1,0:T(8,128)} %get-tuple-element.84), channel_id=1, source_target_pairs={{0,4},{1,5},{2,6},{3,7},{4,0},{5,1},{6,2},{7,3},{8,12},{9,13},{10,... | collective-permute-start | bytes 393224 | tf_op jit(solution)/shard_map/ppermute | solution.py:148
  18.5 15.8 %collective-permute-start.6 = (f32[128,256]{1,0:T(8,128)}, f32[128,256]{1,0:T(8,128)}, u32[]{:S(2)}, u32[]{:S(2)}) collective-permute-start(f32[128,256]{1,0:T(8,128)} %get-tuple-element.85), channel_id=1, source_target_pairs={{0,5},{1,4},{2,7},{3,6},{4,1},{5,0},{6,3},{7,2},{8,13},{9,12},{10,... | collective-permute-start | bytes 393224 | tf_op jit(solution)/shard_map/ppermute | solution.py:148
  31.6 8.8 %collective-permute-start.7 = (f32[128,256]{1,0:T(8,128)}, f32[128,256]{1,0:T(8,128)}, u32[]{:S(2)}, u32[]{:S(2)}) collective-permute-start(f32[128,256]{1,0:T(8,128)} %get-tuple-element.86), channel_id=1, source_target_pairs={{0,6},{1,7},{2,4},{3,5},{4,2},{5,3},{6,0},{7,1},{8,14},{9,15},{10,... | collective-permute-start | bytes 393224 | tf_op jit(solution)/shard_map/ppermute | solution.py:148
  31.7 11.3 %collective-permute-start.8 = (f32[128,256]{1,0:T(8,128)}, f32[128,256]{1,0:T(8,128)}, u32[]{:S(2)}, u32[]{:S(2)}) collective-permute-start(f32[128,256]{1,0:T(8,128)} %get-tuple-element.87), channel_id=1, source_target_pairs={{0,7},{1,6},{2,5},{3,4},{4,3},{5,2},{6,1},{7,0},{8,15},{9,14},{10,... | collective-permute-start | bytes 393224 | tf_op jit(solution)/shard_map/ppermute | solution.py:148
  34.3 28.8 %collective-permute-start.15 = (f32[512,256]{1,0:T(8,128)}, f32[512,256]{1,0:T(8,128)}, u32[]{:S(2)}, u32[]{:S(2)}) collective-permute-start(f32[512,256]{1,0:T(8,128)} %get-tuple-element.97), channel_id=1, source_target_pairs={{0,2},{1,3},{2,0},{3,1},{4,6},{5,7},{6,4},{7,5},{8,10},{9,11},{10,... | collective-permute-start | bytes 1572872 | tf_op jit(solution)/shard_map/ppermute | solution.py:148
  40.4 26.7 %collective-permute-start.16 = (f32[512,256]{1,0:T(8,128)}, f32[512,256]{1,0:T(8,128)}, u32[]{:S(2)}, u32[]{:S(2)}) collective-permute-start(f32[512,256]{1,0:T(8,128)} %get-tuple-element.98), channel_id=1, source_target_pairs={{0,3},{1,2},{2,1},{3,0},{4,7},{5,6},{6,5},{7,4},{8,11},{9,10},{10,... | collective-permute-start | bytes 1572872 | tf_op jit(solution)/shard_map/ppermute | solution.py:148
  48.4 45.3 %collective-permute-start.11 = (f32[768,256]{1,0:T(8,128)}, f32[768,256]{1,0:T(8,128)}, u32[]{:S(2)}, u32[]{:S(2)}) collective-permute-start(f32[768,256]{1,0:T(8,128)} %get-tuple-element.93), channel_id=1, source_target_pairs={{0,1},{1,0},{2,3},{3,2},{4,5},{5,4},{6,7},{7,6},{8,9},{9,8},{10,11... | collective-permute-start | bytes 2359304 | tf_op jit(solution)/shard_map/ppermute | solution.py:148
  48.9 48.8 %collective-permute-start.12 = (f32[768,256]{1,0:T(8,128)}, f32[768,256]{1,0:T(8,128)}, u32[]{:S(2)}, u32[]{:S(2)}) collective-permute-start(f32[768,256]{1,0:T(8,128)} %get-tuple-element.94), channel_id=1, source_target_pairs={{0,2},{1,3},{2,0},{3,1},{4,6},{5,7},{6,4},{7,5},{8,10},{9,11},{10,... | collective-permute-start | bytes 2359304 | tf_op jit(solution)/shard_map/ppermute | solution.py:148
  50.5 47.2 %collective-permute-start.13 = (f32[768,256]{1,0:T(8,128)}, f32[768,256]{1,0:T(8,128)}, u32[]{:S(2)}, u32[]{:S(2)}) collective-permute-start(f32[768,256]{1,0:T(8,128)} %get-tuple-element.95), channel_id=1, source_target_pairs={{0,3},{1,2},{2,1},{3,0},{4,7},{5,6},{6,5},{7,4},{8,11},{9,10},{10,... | collective-permute-start | bytes 2359304 | tf_op jit(solution)/shard_map/ppermute | solution.py:148
  63.1 27.9 %collective-permute-start.9 = (f32[3,4,1,1024]{3,2,1,0:T(1,128)}, f32[3,4,1,1024]{3,2,1,0:T(1,128)}, u32[]{:S(2)}, u32[]{:S(2)}) collective-permute-start(f32[3,4,1,1024]{3,2,1,0:T(1,128)} %pad_maximum_fusion), channel_id=1, source_target_pairs={{0,1},{1,2},{2,3},{4,5},{5,6},{6,7},{8,9},{9,10},{10,11},{12,13},{... | collective-permute-start | bytes 147464 | tf_op jit(solution)/shard_map/ppermute | solution.py:399
  67.1 25.2 %collective-permute-start.10 = (f32[3,4,1,1024]{3,2,1,0:T(1,128)}, f32[3,4,1,1024]{3,2,1,0:T(1,128)}, u32[]{:S(2)}, u32[]{:S(2)}) collective-permute-start(f32[3,4,1,1024]{3,2,1,0:T(1,128)} %pad_maximum_fusion.1), channel_id=1, source_target_pairs={{1,0},{2,1},{3,2},{5,4},{6,5},{7,6},{9,8},{10,9},{11,10},{13,12},{... | collective-permute-start | bytes 147464 | tf_op jit(solution)/shard_map/ppermute | solution.py:399
  107.7 54.8 %collective-permute-start.21 = (f32[4,256,1024]{2,1,0:T(8,128)}, f32[4,256,1024]{2,1,0:T(8,128)}, u32[]{:S(2)}, u32[]{:S(2)}) collective-permute-start(f32[4,256,1024]{2,1,0:T(8,128)} %shard_map.92.refs_4_), channel_id=1, source_target_pairs={{0,4},{1,5},{2,6},{3,7},{4,0},{5,1},{6,2},{7,3},{8,12},{9,13},{10,... | collective-permute-start | bytes 12582920 | tf_op jit(solution)/shard_map/ppermute | solution.py:148
  107.7 11.3 %collective-permute-start.26 = (f32[256,256]{1,0:T(8,128)}, f32[256,256]{1,0:T(8,128)}, u32[]{:S(2)}, u32[]{:S(2)}) collective-permute-start(f32[256,256]{1,0:T(8,128)} %get-tuple-element.113), channel_id=1, source_target_pairs={{0,8},{1,9},{2,10},{3,11},{4,12},{5,13},{6,14},{7,15},{8,0},{9,1},... | collective-permute-start | bytes 786440 | tf_op jit(solution)/shard_map/ppermute | solution.py:148
  110.7 0.6 copy-start
  111.3 3.9 collective-permute-start.17
  111.8 21.1 %collective-permute-start.27 = (f32[256,256]{1,0:T(8,128)}, f32[256,256]{1,0:T(8,128)}, u32[]{:S(2)}, u32[]{:S(2)}) collective-permute-start(f32[256,256]{1,0:T(8,128)} %get-tuple-element.114), channel_id=1, source_target_pairs={{0,16},{1,17},{2,18},{3,19},{4,20},{5,21},{6,22},{7,23},{8,24},{9,... | collective-permute-start | bytes 786440 | tf_op jit(solution)/shard_map/ppermute | solution.py:148
  114.5 24.2 %collective-permute-start.28 = (f32[256,256]{1,0:T(8,128)}, f32[256,256]{1,0:T(8,128)}, u32[]{:S(2)}, u32[]{:S(2)}) collective-permute-start(f32[256,256]{1,0:T(8,128)} %get-tuple-element.115), channel_id=1, source_target_pairs={{0,24},{1,25},{2,26},{3,27},{4,28},{5,29},{6,30},{7,31},{8,16},{9,... | collective-permute-start | bytes 786440 | tf_op jit(solution)/shard_map/ppermute | solution.py:148
  115.2 0.6 copy-start.1
  118.5 24.9 %collective-permute-start.18 = (f32[528,256]{1,0:T(8,128)}, f32[528,256]{1,0:T(8,128)}, u32[]{:S(2)}, u32[]{:S(2)}) collective-permute-start(f32[528,256]{1,0:T(8,128)} %get-tuple-element.106), channel_id=1, source_target_pairs={{0,1},{1,0},{2,3},{3,2},{4,5},{5,4},{6,7},{7,6},{8,9},{9,8},{10,11... | collective-permute-start | bytes 1622024 | tf_op jit(solution)/shard_map/ppermute | solution.py:148
  119.0 21.9 %collective-permute-start.29 = (f32[512,256]{1,0:T(8,128)}, f32[512,256]{1,0:T(8,128)}, u32[]{:S(2)}, u32[]{:S(2)}) collective-permute-start(f32[512,256]{1,0:T(8,128)} %get-tuple-element.116), channel_id=1, source_target_pairs={{0,8},{1,9},{2,10},{3,11},{4,12},{5,13},{6,14},{7,15},{8,0},{9,1},... | collective-permute-start | bytes 1572872 | tf_op jit(solution)/shard_map/ppermute | solution.py:148
  132.9 24.9 %collective-permute-start.19 = (f32[528,256]{1,0:T(8,128)}, f32[528,256]{1,0:T(8,128)}, u32[]{:S(2)}, u32[]{:S(2)}) collective-permute-start(f32[528,256]{1,0:T(8,128)} %get-tuple-element.107), channel_id=1, source_target_pairs={{0,2},{1,3},{2,0},{3,1},{4,6},{5,7},{6,4},{7,5},{8,10},{9,11},{10,... | collective-permute-start | bytes 1622024 | tf_op jit(solution)/shard_map/ppermute | solution.py:148
  138.7 19.5 %collective-permute-start.20 = (f32[528,256]{1,0:T(8,128)}, f32[528,256]{1,0:T(8,128)}, u32[]{:S(2)}, u32[]{:S(2)}) collective-permute-start(f32[528,256]{1,0:T(8,128)} %get-tuple-element.108), channel_id=1, source_target_pairs={{0,3},{1,2},{2,1},{3,0},{4,7},{5,6},{6,5},{7,4},{8,11},{9,10},{10,... | collective-permute-start | bytes 1622024 | tf_op jit(solution)/shard_map/ppermute | solution.py:148
  140.9 120.0 %collective-permute-start.32 = (f32[768,256]{1,0:T(8,128)}, f32[768,256]{1,0:T(8,128)}, u32[]{:S(2)}, u32[]{:S(2)}) collective-permute-start(f32[768,256]{1,0:T(8,128)} %get-tuple-element.119), channel_id=1, source_target_pairs={{0,8},{1,9},{2,10},{3,11},{4,12},{5,13},{6,14},{7,15},{8,0},{9,1},... | collective-permute-start | bytes 2359304 | tf_op jit(solution)/shard_map/ppermute | solution.py:148
  143.4 117.8 %collective-permute-start.33 = (f32[768,256]{1,0:T(8,128)}, f32[768,256]{1,0:T(8,128)}, u32[]{:S(2)}, u32[]{:S(2)}) collective-permute-start(f32[768,256]{1,0:T(8,128)} %get-tuple-element.120), channel_id=1, source_target_pairs={{0,16},{1,17},{2,18},{3,19},{4,20},{5,21},{6,22},{7,23},{8,24},{9,... | collective-permute-start | bytes 2359304 | tf_op jit(solution)/shard_map/ppermute | solution.py:148
  157.8 105.7 %collective-permute-start.34 = (f32[768,256]{1,0:T(8,128)}, f32[768,256]{1,0:T(8,128)}, u32[]{:S(2)}, u32[]{:S(2)}) collective-permute-start(f32[768,256]{1,0:T(8,128)} %get-tuple-element.121), channel_id=1, source_target_pairs={{0,24},{1,25},{2,26},{3,27},{4,28},{5,29},{6,30},{7,31},{8,16},{9,... | collective-permute-start | bytes 2359304 | tf_op jit(solution)/shard_map/ppermute | solution.py:148
  158.2 90.5 %collective-permute-start.30 = (f32[512,256]{1,0:T(8,128)}, f32[512,256]{1,0:T(8,128)}, u32[]{:S(2)}, u32[]{:S(2)}) collective-permute-start(f32[512,256]{1,0:T(8,128)} %get-tuple-element.117), channel_id=1, source_target_pairs={{0,16},{1,17},{2,18},{3,19},{4,20},{5,21},{6,22},{7,23},{8,24},{9,... | collective-permute-start | bytes 1572872 | tf_op jit(solution)/shard_map/ppermute | solution.py:148
  162.4 96.8 %collective-permute-start.31 = (f32[512,256]{1,0:T(8,128)}, f32[512,256]{1,0:T(8,128)}, u32[]{:S(2)}, u32[]{:S(2)}) collective-permute-start(f32[512,256]{1,0:T(8,128)} %get-tuple-element.118), channel_id=1, source_target_pairs={{0,24},{1,25},{2,26},{3,27},{4,28},{5,29},{6,30},{7,31},{8,16},{9,... | collective-permute-start | bytes 1572872 | tf_op jit(solution)/shard_map/ppermute | solution.py:148
  248.6 34.1 %collective-permute-start.38 = (f32[512,256]{1,0:T(8,128)}, f32[512,256]{1,0:T(8,128)}, u32[]{:S(2)}, u32[]{:S(2)}) collective-permute-start(f32[512,256]{1,0:T(8,128)} %get-tuple-element.126), channel_id=1, source_target_pairs={{0,1},{1,0},{2,3},{3,2},{4,5},{5,4},{6,7},{7,6},{8,9},{9,8},{10,11... | collective-permute-start | bytes 1572872 | tf_op jit(solution)/shard_map/ppermute | solution.py:148
  259.3 18.7 %collective-permute-start.41 = (f32[256,256]{1,0:T(8,128)}, f32[256,256]{1,0:T(8,128)}, u32[]{:S(2)}, u32[]{:S(2)}) collective-permute-start(f32[256,256]{1,0:T(8,128)} %get-tuple-element.129), channel_id=1, source_target_pairs={{0,1},{1,0},{2,3},{3,2},{4,5},{5,4},{6,7},{7,6},{8,9},{9,8},{10,11... | collective-permute-start | bytes 786440 | tf_op jit(solution)/shard_map/ppermute | solution.py:148
  260.9 18.9 %collective-permute-start.42 = (f32[256,256]{1,0:T(8,128)}, f32[256,256]{1,0:T(8,128)}, u32[]{:S(2)}, u32[]{:S(2)}) collective-permute-start(f32[256,256]{1,0:T(8,128)} %get-tuple-element.130), channel_id=1, source_target_pairs={{0,2},{1,3},{2,0},{3,1},{4,6},{5,7},{6,4},{7,5},{8,10},{9,11},{10,... | collective-permute-start | bytes 786440 | tf_op jit(solution)/shard_map/ppermute | solution.py:148
  261.2 18.6 %collective-permute-start.43 = (f32[256,256]{1,0:T(8,128)}, f32[256,256]{1,0:T(8,128)}, u32[]{:S(2)}, u32[]{:S(2)}) collective-permute-start(f32[256,256]{1,0:T(8,128)} %get-tuple-element.131), channel_id=1, source_target_pairs={{0,3},{1,2},{2,1},{3,0},{4,7},{5,6},{6,5},{7,4},{8,11},{9,10},{10,... | collective-permute-start | bytes 786440 | tf_op jit(solution)/shard_map/ppermute | solution.py:148
  263.5 5.0 %collective-permute-start.24 = (f32[1,256]{1,0:T(1,128)S(1)}, f32[1,256]{1,0:T(1,128)}, u32[]{:S(2)}, u32[]{:S(2)}) collective-permute-start(f32[1,256]{1,0:T(1,128)S(1)} %get-tuple-element.162), channel_id=1, source_target_pairs={{0,4},{4,8},{8,12},{12,16},{16,20},{20,24},{24,28},{1,5},{5,9},{9,... | collective-permute-start | bytes 3080 | tf_op jit(solution)/shard_map/ppermute | solution.py:399
  268.5 3.2 collective-permute-start.25
  271.7 5.3 %collective-permute-start.22 = (f32[1,256]{1,0:T(1,128)S(1)}, f32[1,256]{1,0:T(1,128)}, u32[]{:S(2)}, u32[]{:S(2)}) collective-permute-start(f32[1,256]{1,0:T(1,128)S(1)} %get-tuple-element.164), channel_id=1, source_target_pairs={{0,4},{4,8},{8,12},{12,16},{16,20},{20,24},{24,28},{1,5},{5,9},{9,... | collective-permute-start | bytes 3080 | tf_op jit(solution)/shard_map/ppermute | solution.py:399
  277.0 25.1 %collective-permute-start.39 = (f32[512,256]{1,0:T(8,128)}, f32[512,256]{1,0:T(8,128)}, u32[]{:S(2)}, u32[]{:S(2)}) collective-permute-start(f32[512,256]{1,0:T(8,128)} %get-tuple-element.127), channel_id=1, source_target_pairs={{0,2},{1,3},{2,0},{3,1},{4,6},{5,7},{6,4},{7,5},{8,10},{9,11},{10,... | collective-permute-start | bytes 1572872 | tf_op jit(solution)/shard_map/ppermute | solution.py:148
  278.0 25.4 %collective-permute-start.40 = (f32[512,256]{1,0:T(8,128)}, f32[512,256]{1,0:T(8,128)}, u32[]{:S(2)}, u32[]{:S(2)}) collective-permute-start(f32[512,256]{1,0:T(8,128)} %get-tuple-element.128), channel_id=1, source_target_pairs={{0,3},{1,2},{2,1},{3,0},{4,7},{5,6},{6,5},{7,4},{8,11},{9,10},{10,... | collective-permute-start | bytes 1572872 | tf_op jit(solution)/shard_map/ppermute | solution.py:148
  279.8 26.6 %collective-permute-start.35 = (f32[528,256]{1,0:T(8,128)}, f32[528,256]{1,0:T(8,128)}, u32[]{:S(2)}, u32[]{:S(2)}) collective-permute-start(f32[528,256]{1,0:T(8,128)} %get-tuple-element.122), channel_id=1, source_target_pairs={{0,8},{1,9},{2,10},{3,11},{4,12},{5,13},{6,14},{7,15},{8,0},{9,1},... | collective-permute-start | bytes 1622024 | tf_op jit(solution)/shard_map/ppermute | solution.py:148
  279.8 39.1 %collective-permute-start.36 = (f32[528,256]{1,0:T(8,128)}, f32[528,256]{1,0:T(8,128)}, u32[]{:S(2)}, u32[]{:S(2)}) collective-permute-start(f32[528,256]{1,0:T(8,128)} %get-tuple-element.123), channel_id=1, source_target_pairs={{0,16},{1,17},{2,18},{3,19},{4,20},{5,21},{6,22},{7,23},{8,24},{9,... | collective-permute-start | bytes 1622024 | tf_op jit(solution)/shard_map/ppermute | solution.py:148
  282.7 46.7 %collective-permute-start.37 = (f32[528,256]{1,0:T(8,128)}, f32[528,256]{1,0:T(8,128)}, u32[]{:S(2)}, u32[]{:S(2)}) collective-permute-start(f32[528,256]{1,0:T(8,128)} %get-tuple-element.124), channel_id=1, source_target_pairs={{0,24},{1,25},{2,26},{3,27},{4,28},{5,29},{6,30},{7,31},{8,16},{9,... | collective-permute-start | bytes 1622024 | tf_op jit(solution)/shard_map/ppermute | solution.py:148
  302.2 32.2 %collective-permute-start.46 = (f32[256,256]{1,0:T(8,128)}, f32[256,256]{1,0:T(8,128)}, u32[]{:S(2)}, u32[]{:S(2)}) collective-permute-start(f32[256,256]{1,0:T(8,128)} %get-tuple-element.139), channel_id=1, source_target_pairs={{0,1},{1,0},{2,3},{3,2},{4,5},{5,4},{6,7},{7,6},{8,9},{9,8},{10,11... | collective-permute-start | bytes 786440 | tf_op jit(solution)/shard_map/ppermute | solution.py:148
  303.3 33.0 %collective-permute-start.47 = (f32[256,256]{1,0:T(8,128)}, f32[256,256]{1,0:T(8,128)}, u32[]{:S(2)}, u32[]{:S(2)}) collective-permute-start(f32[256,256]{1,0:T(8,128)} %get-tuple-element.140), channel_id=1, source_target_pairs={{0,2},{1,3},{2,0},{3,1},{4,6},{5,7},{6,4},{7,5},{8,10},{9,11},{10,... | collective-permute-start | bytes 786440 | tf_op jit(solution)/shard_map/ppermute | solution.py:148
  306.4 31.4 %collective-permute-start.48 = (f32[256,256]{1,0:T(8,128)}, f32[256,256]{1,0:T(8,128)}, u32[]{:S(2)}, u32[]{:S(2)}) collective-permute-start(f32[256,256]{1,0:T(8,128)} %get-tuple-element.141), channel_id=1, source_target_pairs={{0,3},{1,2},{2,1},{3,0},{4,7},{5,6},{6,5},{7,4},{8,11},{9,10},{10,... | collective-permute-start | bytes 786440 | tf_op jit(solution)/shard_map/ppermute | solution.py:148
  318.9 20.0 %collective-permute-start.55 = (f32[256,256]{1,0:T(8,128)}, f32[256,256]{1,0:T(8,128)}, u32[]{:S(2)}, u32[]{:S(2)}) collective-permute-start(f32[256,256]{1,0:T(8,128)} %get-tuple-element.151), channel_id=1, source_target_pairs={{0,8},{1,9},{2,10},{3,11},{4,12},{5,13},{6,14},{7,15},{8,0},{9,1},... | collective-permute-start | bytes 786440 | tf_op jit(solution)/shard_map/ppermute | solution.py:148
  329.4 4.9 %collective-permute-start.23 = (f32[1,256]{1,0:T(1,128)}, f32[1,256]{1,0:T(1,128)}, u32[]{:S(2)}, u32[]{:S(2)}) collective-permute-start(f32[1,256]{1,0:T(1,128)} %get-tuple-element.165), channel_id=1, source_target_pairs={{4,0},{8,4},{12,8},{16,12},{20,16},{24,20},{28,24},{5,1},{9,5},{13... | collective-permute-start | bytes 3080 | tf_op jit(solution)/shard_map/ppermute | solution.py:399
  334.3 57.4 %collective-permute-start.52 = (f32[512,256]{1,0:T(8,128)}, f32[512,256]{1,0:T(8,128)}, u32[]{:S(2)}, u32[]{:S(2)}) collective-permute-start(f32[512,256]{1,0:T(8,128)} %get-tuple-element.148), channel_id=1, source_target_pairs={{0,8},{1,9},{2,10},{3,11},{4,12},{5,13},{6,14},{7,15},{8,0},{9,1},... | collective-permute-start | bytes 1572872 | tf_op jit(solution)/shard_map/ppermute | solution.py:148
  334.4 23.3 %collective-permute-start.56 = (f32[256,256]{1,0:T(8,128)}, f32[256,256]{1,0:T(8,128)}, u32[]{:S(2)}, u32[]{:S(2)}) collective-permute-start(f32[256,256]{1,0:T(8,128)} %get-tuple-element.152), channel_id=1, source_target_pairs={{0,16},{1,17},{2,18},{3,19},{4,20},{5,21},{6,22},{7,23},{8,24},{9,... | collective-permute-start | bytes 786440 | tf_op jit(solution)/shard_map/ppermute | solution.py:148
  336.4 48.4 %collective-permute-start.57 = (f32[256,256]{1,0:T(8,128)}, f32[256,256]{1,0:T(8,128)}, u32[]{:S(2)}, u32[]{:S(2)}) collective-permute-start(f32[256,256]{1,0:T(8,128)} %get-tuple-element.153), channel_id=1, source_target_pairs={{0,24},{1,25},{2,26},{3,27},{4,28},{5,29},{6,30},{7,31},{8,16},{9,... | collective-permute-start | bytes 786440 | tf_op jit(solution)/shard_map/ppermute | solution.py:148
  337.9 68.2 %collective-permute-start.53 = (f32[512,256]{1,0:T(8,128)}, f32[512,256]{1,0:T(8,128)}, u32[]{:S(2)}, u32[]{:S(2)}) collective-permute-start(f32[512,256]{1,0:T(8,128)} %get-tuple-element.149), channel_id=1, source_target_pairs={{0,16},{1,17},{2,18},{3,19},{4,20},{5,21},{6,22},{7,23},{8,24},{9,... | collective-permute-start | bytes 1572872 | tf_op jit(solution)/shard_map/ppermute | solution.py:148
  338.9 79.6 %collective-permute-start.54 = (f32[512,256]{1,0:T(8,128)}, f32[512,256]{1,0:T(8,128)}, u32[]{:S(2)}, u32[]{:S(2)}) collective-permute-start(f32[512,256]{1,0:T(8,128)} %get-tuple-element.150), channel_id=1, source_target_pairs={{0,24},{1,25},{2,26},{3,27},{4,28},{5,29},{6,30},{7,31},{8,16},{9,... | collective-permute-start | bytes 1572872 | tf_op jit(solution)/shard_map/ppermute | solution.py:148
  357.7 32.2 %collective-permute-start.44 = (f32[128,128]{1,0:T(8,128)}, f32[128,128]{1,0:T(8,128)}, u32[]{:S(2)}, u32[]{:S(2)}) collective-permute-start(f32[128,128]{1,0:T(8,128)} %get-tuple-element.137), channel_id=1, source_target_pairs={{0,1},{1,2},{2,3},{4,5},{5,6},{6,7},{8,9},{9,10},{10,11},{12,13},{... | collective-permute-start | bytes 196616 | tf_op jit(solution)/shard_map/ppermute | solution.py:399
  384.7 6.5 %collective-permute-start.45 = (f32[128,128]{1,0:T(8,128)}, f32[128,128]{1,0:T(8,128)}, u32[]{:S(2)}, u32[]{:S(2)}) collective-permute-start(f32[128,128]{1,0:T(8,128)} %get-tuple-element.138), channel_id=1, source_target_pairs={{1,0},{2,1},{3,2},{5,4},{6,5},{7,6},{9,8},{10,9},{11,10},{13,12},{... | collective-permute-start | bytes 196616 | tf_op jit(solution)/shard_map/ppermute | solution.py:399
  389.9 34.3 %collective-permute-start.49 = (f32[256,256]{1,0:T(8,128)}, f32[256,256]{1,0:T(8,128)}, u32[]{:S(2)}, u32[]{:S(2)}) collective-permute-start(f32[256,256]{1,0:T(8,128)} %get-tuple-element.145), channel_id=1, source_target_pairs={{0,8},{1,9},{2,10},{3,11},{4,12},{5,13},{6,14},{7,15},{8,0},{9,1},... | collective-permute-start | bytes 786440 | tf_op jit(solution)/shard_map/ppermute | solution.py:148
  391.2 32.9 %collective-permute-start.50 = (f32[256,256]{1,0:T(8,128)}, f32[256,256]{1,0:T(8,128)}, u32[]{:S(2)}, u32[]{:S(2)}) collective-permute-start(f32[256,256]{1,0:T(8,128)} %get-tuple-element.146), channel_id=1, source_target_pairs={{0,16},{1,17},{2,18},{3,19},{4,20},{5,21},{6,22},{7,23},{8,24},{9,... | collective-permute-start | bytes 786440 | tf_op jit(solution)/shard_map/ppermute | solution.py:148
  391.7 37.2 %collective-permute-start.51 = (f32[256,256]{1,0:T(8,128)}, f32[256,256]{1,0:T(8,128)}, u32[]{:S(2)}, u32[]{:S(2)}) collective-permute-start(f32[256,256]{1,0:T(8,128)} %get-tuple-element.147), channel_id=1, source_target_pairs={{0,24},{1,25},{2,26},{3,27},{4,28},{5,29},{6,30},{7,31},{8,16},{9,... | collective-permute-start | bytes 786440 | tf_op jit(solution)/shard_map/ppermute | solution.py:148
